TPU v7x, 512 devices: a whole 4x8x8 slice. The times are simulated.
512 devices in a mesh: dp: 16 (over z, core), ctx: 32 (over x, y).
Axes of the slice: x: 4, y: 8, z: 8, core: 2. Of those that a mesh axis runs over, the one named last changes fastest.
Arguments:
- signal: bfloat16 [16, 1024, 4096], P('dp', None, 'ctx'), may hold values from -6 to 6
- gate: bfloat16 [16, 1024, 4096], P('dp', None, 'ctx'), may hold values from -6 to 6
- cotangent: bfloat16 [16, 1024, 4096], P('dp', None, 'ctx'), may hold values from -6 to 6
- w_in: bfloat16 [64, 33], replicated, may hold values from -1 to 1
- w_mid: bfloat16 [64, 64], replicated, may hold values from -0.75 to 0.75
- w_out: bfloat16 [1024, 64], replicated, may hold values from -0.75 to 0.75
- rates: float32 [1024], replicated, may hold values from 1 to 30
- skip: float32 [1024], replicated, may hold values from -4 to 4
- lengths: int32 [1024], replicated, may hold values from 32 to 4096
- owner: int32 [1024], replicated, may hold values from 0 to 31, as said below
Outputs:
- result: bfloat16 [16, 1024, 4096], P('dp', None, 'ctx')
- d_gate: bfloat16 [16, 1024, 4096], P('dp', None, 'ctx')
- d_signal: bfloat16 [16, 1024, 4096], P('dp', None, 'ctx')
- tap_grad: float32 [2048, 4096], P('ctx', 'dp')
Inputs may be any that keep to these rules, and one draw needn't show every extreme that they name: `owner`: each index of ctx owns at most 64 channels, and in every draw some index owns exactly 64.
All inputs are finite; a program needn't handle non-finite values.
Results may differ from a plain program's by a relative error of at most 0.0036.
Values may be sent and summed in bfloat16 or wider, within the bound.
No kernel may reach another device: no remote copies, remote signals or barrier semaphores. Data moves between devices by JAX's collectives and lax.ppermute only.
A program may use at most 64 MiB of HBM per device.

v0:
```python
import math

import jax
import jax.numpy as jnp
from jax import lax
from jax.sharding import PartitionSpec as P

PRECISE = lax.Precision.HIGH
COLUMNS = 128


def embed_points(points, seq_total, bands):
    freq_ids = jnp.arange(1, bands + 1, dtype=jnp.int32)
    phase = (freq_ids[:, None] * points[None, :] % seq_total).astype(jnp.float32) * (
        2.0 * math.pi / seq_total
    )
    ramp = points.astype(jnp.float32)[None, :] / seq_total
    return jnp.concatenate([ramp, jnp.cos(phase), jnp.sin(phase)], axis=0).astype(jnp.bfloat16)


def filter_rows(points, w_in, w_mid, w_out_rows, rate_rows, length_rows, seq_total):
    embedded = embed_points(points, seq_total, (w_in.shape[1] - 1) // 2)
    act_one = jnp.sin(jnp.dot(w_in, embedded, preferred_element_type=jnp.float32)).astype(
        jnp.bfloat16
    )
    act_two = jnp.sin(jnp.dot(w_mid, act_one, preferred_element_type=jnp.float32)).astype(
        jnp.bfloat16
    )
    network = jnp.dot(w_out_rows, act_two, preferred_element_type=jnp.float32)
    moments = points.astype(jnp.float32)
    decay = jnp.exp(-rate_rows[:, None] * moments[None, :] / seq_total)
    scaling = lax.rsqrt(length_rows.astype(jnp.float32))
    inside = points[None, :] < length_rows[:, None]
    return jnp.where(inside, network * decay * scaling[:, None], 0.0).astype(jnp.bfloat16)


def slot_layout(owner, holders, capacity):
    onehot = (owner[:, None] == jnp.arange(holders, dtype=jnp.int32)[None, :]).astype(jnp.int32)
    running = jnp.cumsum(onehot, axis=0)
    within = jnp.sum(running * onehot, axis=1) - 1
    slot_pos = owner * capacity + within
    slot_chan = (
        jnp.zeros((holders * capacity,), jnp.int32)
        .at[slot_pos]
        .set(jnp.arange(owner.shape[0], dtype=jnp.int32))
    )
    filled = jnp.zeros((holders * capacity,), jnp.float32).at[slot_pos].set(1.0)
    return (slot_pos, slot_chan, filled)


def dft_tables(length_two):
    row_count = length_two // COLUMNS
    half_rows = row_count // 2
    row_ids = jnp.arange(row_count, dtype=jnp.int32)
    col_ids = jnp.arange(COLUMNS, dtype=jnp.int32)
    half_ids = jnp.arange(half_rows, dtype=jnp.int32)
    first_angle = (row_ids[:, None] * half_ids[None, :] % row_count).astype(jnp.float32) * (
        2.0 * math.pi / row_count
    )
    twist_angle = (row_ids[:, None] * col_ids[None, :] % length_two).astype(jnp.float32) * (
        2.0 * math.pi / length_two
    )
    second_angle = (col_ids[:, None] * col_ids[None, :] % COLUMNS).astype(jnp.float32) * (
        2.0 * math.pi / COLUMNS
    )
    return (
        jnp.cos(first_angle),
        jnp.sin(first_angle),
        jnp.cos(twist_angle),
        jnp.sin(twist_angle),
        jnp.cos(second_angle),
        jnp.sin(second_angle),
    )


def forward_dft(values, tables):
    cos_first, sin_first, cos_twist, sin_twist, cos_second, sin_second = tables
    real_one = jnp.einsum("kn,cnm->ckm", cos_first, values, precision=PRECISE)
    imag_one = -jnp.einsum("kn,cnm->ckm", sin_first, values, precision=PRECISE)
    real_two = real_one * cos_twist + imag_one * sin_twist
    imag_two = imag_one * cos_twist - real_one * sin_twist
    real_out = jnp.einsum("ckm,mj->ckj", real_two, cos_second, precision=PRECISE) + jnp.einsum(
        "ckm,mj->ckj", imag_two, sin_second, precision=PRECISE
    )
    imag_out = jnp.einsum("ckm,mj->ckj", imag_two, cos_second, precision=PRECISE) - jnp.einsum(
        "ckm,mj->ckj", real_two, sin_second, precision=PRECISE
    )
    return (real_out, imag_out)


def inverse_dft(spectrum, tables, length_two):
    cos_first, sin_first, cos_twist, sin_twist, cos_second, sin_second = tables
    real_in, imag_in = spectrum
    real_one = jnp.einsum("ckj,jm->ckm", real_in, cos_second, precision=PRECISE) - jnp.einsum(
        "ckj,jm->ckm", imag_in, sin_second, precision=PRECISE
    )
    imag_one = jnp.einsum("ckj,jm->ckm", imag_in, cos_second, precision=PRECISE) + jnp.einsum(
        "ckj,jm->ckm", real_in, sin_second, precision=PRECISE
    )
    real_two = real_one * cos_twist - imag_one * sin_twist
    imag_two = imag_one * cos_twist + real_one * sin_twist
    joined = jnp.einsum("kn,ckm->cnm", cos_first, real_two, precision=PRECISE) - jnp.einsum(
        "kn,ckm->cnm", sin_first, imag_two, precision=PRECISE
    )
    return joined / length_two


def spectral_product(left, right, conjugate):
    left_real, left_imag = left
    right_real, right_imag = right
    if conjugate:
        right_imag = -right_imag
    return (
        left_real * right_real - left_imag * right_imag,
        left_real * right_imag + left_imag * right_real,
    )


def convolve_block(
    sig_rows, gate_rows, cot_rows, tap_rows, skip_rows, length_rows, tables, norm_factor
):
    block_rows, seq_len = sig_rows.shape
    length_two = 2 * seq_len
    folded = (block_rows, length_two // COLUMNS // 2, COLUMNS)
    sig_wide = sig_rows.astype(jnp.float32)
    gate_wide = gate_rows.astype(jnp.float32)
    cot_wide = cot_rows.astype(jnp.float32)
    back = cot_wide * gate_wide
    sig_spec = forward_dft(sig_wide.reshape(folded), tables)
    tap_spec = forward_dft(tap_rows.astype(jnp.float32).reshape(folded), tables)
    back_spec = forward_dft(back.reshape(folded), tables)
    conv = inverse_dft(spectral_product(sig_spec, tap_spec, False), tables, length_two).reshape(
        block_rows, seq_len
    )
    spread = inverse_dft(spectral_product(back_spec, tap_spec, True), tables, length_two).reshape(
        block_rows, seq_len
    )
    corr = inverse_dft(spectral_product(back_spec, sig_spec, True), tables, length_two).reshape(
        block_rows, seq_len
    )
    mixed = conv + skip_rows[:, None] * sig_wide
    outputs = jnp.stack(
        [
            (gate_wide * mixed).astype(jnp.bfloat16),
            (cot_wide * mixed).astype(jnp.bfloat16),
            (skip_rows[:, None] * back + spread).astype(jnp.bfloat16),
        ]
    )
    inside = jnp.arange(seq_len, dtype=jnp.int32)[None, :] < length_rows[:, None]
    tap_piece = jnp.where(inside, corr * norm_factor, 0.0)
    return (outputs, tap_piece)


def run_blocks(sig_all, gate_all, cot_all, tap_all, skip_rows, length_rows, norm_factor):
    chan_total, seq_len = sig_all.shape
    block_rows = math.gcd(chan_total, 8)
    tables = dft_tables(2 * seq_len)

    def one_block(block_id, state_pair):
        results, gradients = state_pair
        offset = block_id * block_rows

        def window(array):
            return lax.dynamic_slice_in_dim(array, offset, block_rows, 0)

        outputs, tap_piece = convolve_block(
            window(sig_all),
            window(gate_all),
            window(cot_all),
            window(tap_all),
            window(skip_rows),
            window(length_rows),
            tables,
            norm_factor,
        )
        results = lax.dynamic_update_slice_in_dim(results, outputs, offset, 1)
        gradients = lax.dynamic_update_slice_in_dim(gradients, tap_piece, offset, 0)
        return (results, gradients)

    initial = (
        jnp.zeros((3, chan_total, seq_len), jnp.bfloat16),
        jnp.zeros((chan_total, seq_len), jnp.float32),
    )
    return lax.fori_loop(0, chan_total // block_rows, one_block, initial)


def shards(signal, gate, cotangent, w_in, w_mid, w_out, rates, skip, lengths, owner):
    ctx_count = lax.axis_size("ctx")
    ctx_place = lax.axis_index("ctx")
    local_len = signal.shape[2]
    channels = signal.shape[1]
    seq_len = local_len * ctx_count
    sequences = signal.shape[0] * lax.axis_size("dp")
    norm_factor = 1.0 / math.sqrt(seq_len * sequences)
    per_owner = channels // ctx_count
    capacity = 2 * per_owner
    slot_pos, slot_chan, filled = slot_layout(owner, ctx_count, capacity)
    mine = lax.dynamic_slice_in_dim(slot_chan, ctx_place * capacity, capacity)
    members = [signal[0], gate[0], cotangent[0]]
    points = ctx_place * local_len + jnp.arange(local_len, dtype=jnp.int32)
    members.append(filter_rows(points, w_in, w_mid, w_out, rates, lengths, seq_len))
    stacked = jnp.stack(members)
    outgoing = stacked[:, slot_chan, :] * filled[None, :, None].astype(jnp.bfloat16)
    arrived = lax.all_to_all(outgoing, "ctx", split_axis=1, concat_axis=2, tiled=True)
    tap_all = arrived[3]
    results, gradients = run_blocks(
        arrived[0], arrived[1], arrived[2], tap_all, skip[mine], lengths[mine], norm_factor
    )
    returned = lax.all_to_all(results, "ctx", split_axis=2, concat_axis=1, tiled=True)
    outputs = returned[:, slot_pos, :]
    tap_grad = lax.psum_scatter(gradients, "dp", scatter_dimension=1, tiled=True)
    return (outputs[0][None], outputs[1][None], outputs[2][None], tap_grad)


def solution(mesh):
    return jax.shard_map(
        shards,
        mesh=mesh,
        in_specs=(
            P("dp", None, "ctx"),
            P("dp", None, "ctx"),
            P("dp", None, "ctx"),
            P(),
            P(),
            P(),
            P(),
            P(),
            P(),
            P(),
        ),
        out_specs=(
            P("dp", None, "ctx"),
            P("dp", None, "ctx"),
            P("dp", None, "ctx"),
            P("ctx", "dp"),
        ),
        check_vma=False,
    )
```

profile of v0, /device:TPU:1, one launch (start us, length us, event | category | flops | bytes accessed | tf_op | source)
XLA Modules:
  0.0 366.8 jit_solution(14038678024361018827)
XLA Ops:
  8.6 1.1 copy.56
  9.7 1.1 copy.57
  10.8 1.1 copy.58
  13.1 1.2 fusion.328
  15.3 9.0 %reduce-window.6 = s32[32,8,128]{2,1,0:T(8,128)S(1)} reduce-window(s32[32,8,128]{2,1,0:T(8,128)S(1)} %fusion.333, s32[]{:T(128)} %constant.134.clone.1), window={size=1x1x128 pad=0_0x0_0x127_0}, to_apply=%region_0.0 | reduce-window | flops 4161536 | bytes 262148 | tf_op jit(solution)/shard_map/reduce-window
  24.8 4.3 %scatter_custom_fusion = s32[2048]{0:T(1024)S(1)} fusion(s32[1024]{0:T(1024)S(1)} %get-tuple-element.566, s32[1024]{0:T(1024)S(1)} %iota.52, s32[]{:T(128)} %constant.134.clone.1), kind=kCustom, calls=%fused_computation.384 | custom fusion | bytes 8196 | tf_op jit(solution)/shard_map/scatter | solution.py:45
  29.2 4.3 %scatter_custom_fusion.1 = f32[2048]{0:T(1024)S(1)} fusion(s32[1024]{0:T(1024)S(1)} %get-tuple-element.566, f32[1024]{0:T(1024)S(1)} %broadcast.136, f32[]{:T(128)} %constant.136.clone.1), kind=kCustom, calls=%fused_computation.382 | custom fusion | bytes 8196 | tf_op jit(solution)/shard_map/scatter | solution.py:47
  33.5 6.8 %gather_fusion = bf16[2048,4,128]{2,1,0:T(4,128)(2,1)S(1)} fusion(bf16[4,1024,128]{2,0,1:T(4,128)(2,1)S(1)} %copy.61, s32[2048]{0:T(1024)S(1)} %fusion.342), kind=kCustom, calls=%fused_computation | custom fusion | bytes 4202496 | tf_op jit(solution)/shard_map/gather | solution.py:203
  40.3 8.3 %multiply_bitcast_fusion = bf16[4,2048,128]{2,0,1:T(4,128)(2,1)} fusion(bf16[2048,4,128]{2,1,0:T(4,128)(2,1)S(1)} %gather_fusion, bf16[2048]{0:T(1024)(128)(2,1)S(1)} %convert_element_type.219), kind=kLoop, calls=%fused_computation.340 | loop fusion | flops 1048576 | bytes 4198400 | tf_op jit(solution)/shard_map/mul | solution.py:203
  48.6 10.6 %all-to-all-start = ((bf16[4,2048,128]{2,0,1:T(4,128)(2,1)}), bf16[4,2048,128]{2,0,1:T(4,128)(2,1)S(1)}, u32[]{:S(2)}, u32[]{:S(2)}) async-start(bf16[4,2048,128]{2,0,1:T(4,128)(2,1)} %multiply_bitcast_fusion), calls=%async_computation | async-start | bytes 4194304 | tf_op jit(solution)/shard_map/all_to_all | solution.py:204
  60.8 47.3 %all-to-all-done = bf16[4,2048,128]{2,0,1:T(4,128)(2,1)S(1)} async-done(((bf16[4,2048,128]{2,0,1:T(4,128)(2,1)}), bf16[4,2048,128]{2,0,1:T(4,128)(2,1)S(1)}, u32[]{:S(2)}, u32[]{:S(2)}) %all-to-all-start) | async-done | bytes 2097184 | tf_op jit(solution)/shard_map/all_to_all | solution.py:204
  113.5 159.4 %while.17 = (s32[]{:T(128)}, bf16[3,64,4096]{2,1,0:T(8,128)(2,1)S(1)}, f32[64,4096]{1,0:T(8,128)S(1)}, bf16[64,4096]{1,0:T(8,128)(2,1)}, bf16[64,4096]{1,0:T(8,1...) while((s32[]{:T(128)}, ...), condition=%wide.region_6.7_spmd.clone.clone, body=%wide.region_5.6_spmd.clone.clone.sunk | while | flops 1372127232 | bytes 30999400 | solution.py:184
  132.5 1.1 fusion.529
  152.4 1.1 fusion.529
  272.9 4.7 %copy.67 = bf16[3,64,4096]{1,0,2:T(4,128)(2,1)} copy(bf16[3,64,4096]{2,1,0:T(8,128)(2,1)S(1)} %get-tuple-element.411) | data formatting | bytes 3145728 | tf_op jit(solution)/shard_map/while | solution.py:184
  277.7 7.2 %reshape.175 = bf16[32,2,12288]{2,1,0:T(2,128)(2,1)} reshape(bf16[4096,3,64]{2,1,0:T(4,128)(2,1)} %bitcast.351) | data formatting | bytes 3145728
  284.9 7.0 %all-to-all-start.1 = ((bf16[32,2,12288]{2,1,0:T(2,128)(2,1)}), bf16[32,2,12288]{2,1,0:T(2,128)(2,1)S(1)}, u32[]{:S(2)}, u32[]{:S(2)}) async-start(bf16[32,2,12288]{2,1,0:T(2,128)(2,1)} %reshape.175), calls=%async_computation.1 | async-start | bytes 3145728 | tf_op jit(solution)/shard_map/all_to_all | solution.py:209
  292.7 35.9 %all-to-all-done.1 = bf16[32,2,12288]{2,1,0:T(2,128)(2,1)S(1)} async-done(((bf16[32,2,12288]{2,1,0:T(2,128)(2,1)}), bf16[32,2,12288]{2,1,0:T(2,128)(2,1)S(1)}, u32[]{:S(2)}, u32[]{:S(2)}) %all-to-all-start.1) | async-done | bytes 1572896 | tf_op jit(solution)/shard_map/all_to_all | solution.py:209
  328.5 4.7 %reshape.176 = bf16[4096,3,64]{2,1,0:T(4,128)(2,1)} reshape(bf16[32,2,12288]{2,1,0:T(2,128)(2,1)S(1)} %all-to-all-done.1) | data formatting | bytes 3145728
  333.3 5.8 %copy.75 = bf16[3,64,32,128]{3,1,2,0:T(8,128)(2,1)S(1)} copy(bf16[3,64,32,128]{1,0,3,2:T(4,128)(2,1)} %bitcast.352) | data formatting | bytes 3145728 | tf_op jit(solution)/shard_map/all_to_all | solution.py:209
  339.1 10.8 %copy.70 = bf16[3,2048,128]{2,0,1:T(4,128)(2,1)} copy(bf16[3,2048,128]{2,1,0:T(8,128)(2,1)S(1)} %bitcast.354) | data formatting | bytes 3145728 | tf_op jit(solution)/shard_map/all_to_all | solution.py:209
  349.9 5.1 %gather_fusion.3 = bf16[1024,3,128]{2,1,0:T(4,128)(2,1)S(1)} fusion(bf16[3,2048,128]{2,0,1:T(4,128)(2,1)} %copy.70, s32[1024]{0:T(1024)S(1)} %get-tuple-element.565), kind=kCustom, calls=%fused_computation.3 | custom fusion | bytes 1576960 | tf_op jit(solution)/shard_map/gather | solution.py:210
  355.0 1.1 fusion.350
  358.4 1.6 reduce-scatter.2.cloned.1.call-done
  (403 shorter events, 168.5 us)
Async XLA Ops:
  7.2 5.9 %copy-start = (bf16[1024,64]{0,1:T(8,128)(2,1)S(1)}, bf16[1024,64]{0,1:T(8,128)(2,1)}, u32[]{:S(2)}) copy-start(bf16[1024,64]{0,1:T(8,128)(2,1)} %param.17) | copy-start | bytes 393220
  14.3 0.9 copy-start.4
  48.6 10.7 %copy-start.1 = (s32[1024]{0:T(1024)S(1)}, s32[1024]{0:T(1024)}, u32[]{:S(2)}) copy-start(s32[1024]{0:T(1024)} %param.20) | copy-start | bytes 12292
  48.6 11.5 %copy-start.2 = (f32[1024]{0:T(1024)S(1)}, f32[1024]{0:T(1024)}, u32[]{:S(2)}) copy-start(f32[1024]{0:T(1024)} %param.19) | copy-start | bytes 12292
  48.6 59.5 %all-to-all-start = ((bf16[4,2048,128]{2,0,1:T(4,128)(2,1)}), bf16[4,2048,128]{2,0,1:T(4,128)(2,1)S(1)}, u32[]{:S(2)}, u32[]{:S(2)}) async-start(bf16[4,2048,128]{2,0,1:T(4,128)(2,1)} %multiply_bitcast_fusion), calls=%async_computation | async-start | bytes 4194304 | tf_op jit(solution)/shard_map/all_to_all | solution.py:204
  272.9 4.8 %copy-start.3 = (f32[64,4096]{1,0:T(8,128)}, f32[64,4096]{1,0:T(8,128)S(1)}, u32[]{:S(2)}) copy-start(f32[64,4096]{1,0:T(8,128)S(1)} %get-tuple-element.412) | copy-start | bytes 3145732
  284.9 43.6 %all-to-all-start.1 = ((bf16[32,2,12288]{2,1,0:T(2,128)(2,1)}), bf16[32,2,12288]{2,1,0:T(2,128)(2,1)S(1)}, u32[]{:S(2)}, u32[]{:S(2)}) async-start(bf16[32,2,12288]{2,1,0:T(2,128)(2,1)} %reshape.175), calls=%async_computation.1 | async-start | bytes 3145728 | tf_op jit(solution)/shard_map/all_to_all | solution.py:209
  291.9 68.0 %reduce-scatter.2.cloned.1.call-start = ((), (), s32[]{:S(2)}) async-start(), calls=%async_computation.3 | async-start | bytes 1114112 | tf_op jit(solution)/shard_map/reduce_scatter | solution.py:211
Sparse Core Ops, SparseCore 0:
  296.1 63.7 reduce-scatter.1
where the time goes:
time: 371 us; the launch traced here: 367 us
  matrix products  133 us (36%)
  waiting for transfers between devices  85.5 us (23%)
  local copies, waits for them, and re-layouts  76.7 us (21%)
  other arithmetic  36.7 us (10%)
  starting transfers between devices  17.7 us (5%)
  between operations  14.4 us (4%)
    all_to_all x1, waiting for transfers between devices, shards(): lax.all_to_all(outgoing, 'ctx', split_axis=1, concat_axis=2, tiled=True)  47.3 us
    all_to_all x1, waiting for transfers between devices, shards(): lax.all_to_all(results, 'ctx', split_axis=2, concat_axis=1, tiled=True)  35.9 us
    unnamed x22, local copies, waits for them, and re-layouts  20.7 us
    all_to_all x2, local copies, waits for them, and re-layouts, shards(): lax.all_to_all(results, 'ctx', split_axis=2, concat_axis=1, tiled=True)  16.6 us
    dot_general x24, matrix products, forward_dft(): jnp.einsum('ckm,mj->ckj', real_two, sin_second, precision=PRECISE)  13.4 us
    dot_general x24, matrix products, forward_dft(): jnp.einsum('ckm,mj->ckj', imag_two, sin_second, precision=PRECISE)  12.4 us
    dot_general x24, matrix products, forward_dft(): jnp.einsum('ckm,mj->ckj', real_two, cos_second, precision=PRECISE)  12.2 us
    dot_general x24, matrix products, forward_dft(): jnp.einsum('ckm,mj->ckj', imag_two, cos_second, precision=PRECISE)  12.1 us
  transfers between devices with their start and end apart: 3, of which 3 were waited for; matrix products, arithmetic and copies ran while one was open for 9% of the time, Pallas kernels for 0%

commit v1 on v0

v1 whole, which is shorter than its diff:
```python
import math

import numpy as np

import jax
import jax.numpy as jnp
import ml_dtypes
from jax import lax
from jax.experimental import pallas as pl
from jax.experimental.pallas import tpu as pltpu
from jax.sharding import PartitionSpec as P

LANES = 128
GROUP = 4
VMEM_LIMIT = 48 * 1024 * 1024


def embed_table(seq_total, features):
    bands = (features - 1) // 2
    points = np.arange(seq_total, dtype=np.int64)
    freq_ids = np.arange(1, bands + 1, dtype=np.int64)
    phase = (freq_ids[:, None] * points[None, :] % seq_total).astype(np.float32) * np.float32(
        2.0 * math.pi / seq_total
    )
    ramp = points.astype(np.float32)[None, :] / np.float32(seq_total)
    table = np.concatenate([ramp, np.cos(phase), np.sin(phase)], axis=0)
    return table.astype(ml_dtypes.bfloat16)


def sine(x):
    turns = jnp.round(x * (1.0 / math.pi))
    r = x - turns * 3.140625
    r = r - turns * 9.67502593994140625e-4
    r = r - turns * 1.509957990978376432e-7
    half = turns * 0.5
    sign = 1.0 - 4.0 * (half - jnp.floor(half))
    s = r * r
    p = -1.0 / 39916800.0
    p = p * s + 1.0 / 362880.0
    p = p * s - 1.0 / 5040.0
    p = p * s + 1.0 / 120.0
    p = p * s - 1.0 / 6.0
    return sign * (r + r * s * p)


def taps_body(emb_ref, w_in_ref, w_mid_ref, w_out_ref, rate_ref, scale_ref, len_ref, out_ref, *, seq_len, width):
    rows = w_out_ref.shape[0]
    out_ref[0:rows, :] = jnp.zeros((rows, LANES), jnp.float32)
    w_in = w_in_ref[...]
    w_mid = w_mid_ref[...]
    w_out = w_out_ref[...]
    for part in range(seq_len // width):
        emb = emb_ref[:, part * width : (part + 1) * width]
        one = sine(jnp.dot(w_in, emb, preferred_element_type=jnp.float32)).astype(jnp.bfloat16)
        two = sine(jnp.dot(w_mid, one, preferred_element_type=jnp.float32)).astype(jnp.bfloat16)
        net = jnp.dot(w_out, two, preferred_element_type=jnp.float32)
        point = part * width + lax.broadcasted_iota(jnp.int32, (rows, width), 1)
        decay = jnp.exp(-rate_ref[...] * point.astype(jnp.float32) / seq_len)
        value = jnp.where(point < len_ref[...], net * decay * scale_ref[...], 0.0)
        value = value.astype(jnp.bfloat16).astype(jnp.float32)
        for sub in range(width // LANES):
            block = part * (width // LANES) + sub + 1
            out_ref[block * rows : (block + 1) * rows, :] = value[:, sub * LANES : (sub + 1) * LANES]


def make_taps(emb, w_in, w_mid, w_out_rows, rate_rows, length_rows, seq_len):
    rows = w_out_rows.shape[0]
    blocks = seq_len // LANES
    body = lambda *refs: taps_body(*refs, seq_len=seq_len, width=512)
    return pl.pallas_call(
        body,
        out_shape=jax.ShapeDtypeStruct(((blocks + 1) * rows, LANES), jnp.float32),
        compiler_params=pltpu.CompilerParams(vmem_limit_bytes=VMEM_LIMIT),
        name="taps",
    )(
        emb,
        w_in,
        w_mid,
        w_out_rows,
        rate_rows[:, None],
        lax.rsqrt(length_rows.astype(jnp.float32))[:, None],
        length_rows[:, None],
    )


def convolve_body(
    len_ref, arr_ref, tap_ref, out_ref, grad_ref,
    wide, flipped, xbuf, bbuf, fbuf, y_wide, z_wide, f_wide, g_prev, *, norm
):
    blocks, pair, _ = arr_ref.shape
    rows = pair // 2
    f32 = jnp.float32
    b16 = jnp.bfloat16
    flip = (
        lax.broadcasted_iota(jnp.int32, (LANES, LANES), 0)
        + lax.broadcasted_iota(jnp.int32, (LANES, LANES), 1)
        == LANES - 1
    ).astype(f32).astype(b16)
    wide[...] = arr_ref[...].reshape(blocks * pair, LANES).astype(f32)
    flipped[...] = jnp.dot(
        arr_ref[...].reshape(blocks * pair, LANES), flip, preferred_element_type=f32
    )
    f_wide[...] = jnp.zeros(f_wide.shape, f32)
    zero = jnp.zeros((blocks, LANES), f32)
    xbuf[0:blocks, :] = zero
    bbuf[blocks : 2 * blocks, :] = zero
    fbuf[blocks : 2 * blocks, :] = zero
    lane = lax.broadcasted_iota(jnp.int32, (8, LANES), 1)
    sub = lax.broadcasted_iota(jnp.int32, (8, LANES), 0)
    build_key = jnp.where(lane >= sub, lane, lane + LANES)
    sum_key = lane + sub

    def channel(c, carry):
        length = len_ref[c]
        xbuf[blocks : 2 * blocks, :] = wide[pl.ds(c, blocks, stride=pair), :]
        bbuf[0:blocks, :] = wide[pl.ds(rows + c, blocks, stride=pair), :]
        fbuf[0:blocks, :] = flipped[pl.ds(rows + c, blocks, stride=pair), :]
        xt = flipped[pl.ds(c, blocks, stride=pair), :].T.astype(b16)
        steps = jnp.minimum((length + LANES - 1) // LANES + 1, blocks)
        groups = (steps + GROUP - 1) // GROUP

        def diagonal(upper, lower):
            total = None
            for a in range(LANES // 8):
                piece = jnp.where(sum_key >= LANES - 1 - 8 * a, upper[8 * a : 8 * a + 8, :], lower[8 * a : 8 * a + 8, :])
                if a:
                    piece = pltpu.roll(piece, 8 * a, 1)
                total = piece if total is None else total + piece
            total = pltpu.roll(total, 1, 1, stride=1, stride_axis=0)
            return jnp.sum(total, axis=0, keepdims=True)

        def put(k, value):
            spot = k * LANES + lax.broadcasted_iota(jnp.int32, (1, LANES), 1)
            f_wide[pl.ds((k + 1) * rows + c, 1), :] = jnp.where(spot < length, value * norm, 0.0)

        def group(g, acc):
            first = g * GROUP
            heads = []
            for j in range(-1, GROUP):
                row = tap_ref[pl.ds((first + j + 1) * rows + c, 1), :]
                heads.append(pltpu.roll(jnp.broadcast_to(row, (8, LANES)), 0, 1, stride=1, stride_axis=0))
            built = []
            left = []
            right = []
            for j in range(GROUP):
                for a in range(LANES // 8):
                    piece = jnp.where(build_key >= LANES - 8 * a, heads[j], heads[j + 1])
                    built.append(pltpu.roll(piece, 8 * a, 1) if a else piece)
                left.append(
                    jnp.concatenate(
                        [xbuf[pl.ds(blocks - first - j, blocks), :], fbuf[pl.ds(first + j, blocks), :]], axis=0
                    ).astype(b16)
                )
                right.append(bbuf[pl.ds(first + j, blocks), :].astype(b16))
            toeplitz = jnp.concatenate(built, axis=0).astype(b16)
            acc = acc + jnp.dot(jnp.concatenate(left, axis=1), toeplitz, preferred_element_type=f32)
            outer = jnp.dot(xt, jnp.concatenate(right, axis=1), preferred_element_type=f32)
            before = g_prev[...]
            for j in range(GROUP):
                now = outer[:, j * LANES : (j + 1) * LANES]
                put(first + j - 1, diagonal(before, now))
                before = now
            g_prev[...] = before
            return acc

        acc = lax.fori_loop(0, groups, group, jnp.zeros((2 * blocks, LANES), f32))

        @pl.when(groups * GROUP == blocks)
        def _():
            last = g_prev[...]
            put(blocks - 1, diagonal(last, jnp.zeros_like(last)))

        y_wide[pl.ds(c, blocks, stride=rows), :] = acc[0:blocks, :]
        z_wide[pl.ds(c, blocks, stride=rows), :] = acc[blocks:, :]
        return carry

    lax.fori_loop(0, rows, channel, 0)
    out_ref[:, 0:rows, :] = y_wide[...].astype(b16).reshape(blocks, rows, LANES)
    out_ref[:, rows:, :] = (
        jnp.dot(z_wide[...].astype(b16), flip, preferred_element_type=f32).astype(b16).reshape(blocks, rows, LANES)
    )
    grad_ref[...] = f_wide[rows:, :].reshape(blocks, rows, LANES)


def convolve(length_rows, arrived, taps, norm):
    blocks, pair, _ = arrived.shape
    rows = pair // 2
    body = lambda *refs: convolve_body(*refs, norm=norm)
    vm = pl.BlockSpec(memory_space=pltpu.VMEM)
    wide = lambda n: pltpu.VMEM((n, LANES), jnp.float32)
    return pl.pallas_call(
        body,
        in_specs=[pl.BlockSpec(memory_space=pltpu.SMEM), vm, vm],
        out_specs=(vm, vm),
        out_shape=(
            jax.ShapeDtypeStruct((blocks, pair, LANES), jnp.bfloat16),
            jax.ShapeDtypeStruct((blocks, rows, LANES), jnp.float32),
        ),
        scratch_shapes=[
            wide(blocks * pair),
            wide(blocks * pair),
            wide(2 * blocks),
            wide(2 * blocks),
            wide(2 * blocks),
            wide(blocks * rows),
            wide(blocks * rows),
            wide((blocks + 1) * rows),
            wide(LANES),
        ],
        compiler_params=pltpu.CompilerParams(vmem_limit_bytes=VMEM_LIMIT),
        name="convolve",
    )(length_rows, arrived, taps)


def pick_body(me_ref, owner_ref, all_ref, out_ref):
    holders, cols, rows, _ = all_ref.shape
    f32 = jnp.float32
    b16 = jnp.bfloat16
    mine = (owner_ref[...] == me_ref[0]).astype(f32)
    lines = mine.shape[0]
    above = lax.broadcasted_iota(jnp.int32, (LANES, LANES), 0) < lax.broadcasted_iota(
        jnp.int32, (LANES, LANES), 1
    )
    within = jnp.dot(mine.astype(b16), above.astype(f32).astype(b16), preferred_element_type=f32)
    counts = jnp.sum(mine, axis=1, keepdims=True)
    slots = out_ref.shape[0]
    slot_id = lax.broadcasted_iota(jnp.int32, (slots, LANES), 0).astype(f32)
    start = jnp.zeros((1, 1), f32)
    pieces = []
    for line in range(lines):
        rank = within[line : line + 1, :] + start
        hit = (slot_id == rank) & (mine[line : line + 1, :] > 0.5)
        pieces.append(hit.astype(f32).astype(b16))
        start = start + counts[line : line + 1, :]
    chosen = jnp.concatenate(pieces, axis=1)
    for col in range(cols):
        table = all_ref[:, col, :, :].reshape(holders * rows, LANES)
        out_ref[:, col * LANES : (col + 1) * LANES] = jnp.dot(chosen, table, preferred_element_type=f32)


def pick_rows(me, owner, everyone, slots):
    holders, cols, rows, _ = everyone.shape
    vm = pl.BlockSpec(memory_space=pltpu.VMEM)
    return pl.pallas_call(
        pick_body,
        in_specs=[pl.BlockSpec(memory_space=pltpu.SMEM), vm, vm],
        out_specs=vm,
        out_shape=jax.ShapeDtypeStruct((slots, cols * LANES), jnp.float32),
        compiler_params=pltpu.CompilerParams(vmem_limit_bytes=VMEM_LIMIT),
        name="pick",
    )(me, owner.reshape(-1, LANES), everyone)


def shards(signal, gate, cotangent, w_in, w_mid, w_out, rates, skip, lengths, owner):
    ctx_count = lax.axis_size("ctx")
    place = lax.axis_index("ctx")
    channels, local_len = signal.shape[1:]
    seq_len = local_len * ctx_count
    sequences = signal.shape[0] * lax.axis_size("dp")
    norm = 1.0 / math.sqrt(seq_len * sequences)
    rows = channels // ctx_count
    f32 = jnp.float32
    b16 = jnp.bfloat16

    sig, gat, cot = signal[0], gate[0], cotangent[0]
    back = cot.astype(f32) * gat.astype(f32)
    outgoing = jnp.concatenate(
        [sig.reshape(ctx_count, rows, local_len), back.astype(b16).reshape(ctx_count, rows, local_len)], axis=1
    )
    arrived = lax.all_to_all(outgoing, "ctx", split_axis=0, concat_axis=0, tiled=True)

    def own(array):
        return lax.dynamic_slice_in_dim(array, place * rows, rows, 0)

    features = w_in.shape[1]
    padded = -(-features // 16) * 16
    table = np.zeros((padded, seq_len), ml_dtypes.bfloat16)
    table[:features] = embed_table(seq_len, features)
    w_in_wide = jnp.pad(w_in, ((0, 0), (0, padded - features)))
    own_lengths = own(lengths)
    taps = make_taps(jnp.asarray(table), w_in_wide, w_mid, own(w_out), own(rates), own_lengths, seq_len)

    outs, grads = convolve(own_lengths, arrived, taps, norm)
    mine = lax.psum_scatter(grads, "dp", scatter_dimension=0, tiled=True)
    everyone = lax.all_gather(mine.astype(b16), "ctx", axis=0, tiled=False)
    returned = lax.all_to_all(outs, "ctx", split_axis=0, concat_axis=0, tiled=True)
    conv = returned[:, :rows, :].reshape(channels, local_len).astype(f32)
    spread = returned[:, rows:, :].reshape(channels, local_len).astype(f32)
    mixed = conv + skip[:, None] * sig.astype(f32)
    result = (gat.astype(f32) * mixed).astype(b16)
    d_gate = (cot.astype(f32) * mixed).astype(b16)
    d_signal = (skip[:, None] * back + spread).astype(b16)
    tap_grad = pick_rows(place.reshape(1).astype(jnp.int32), owner, everyone, 2 * rows)
    return (result[None], d_gate[None], d_signal[None], tap_grad)


def solution(mesh):
    data = P("dp", None, "ctx")
    return jax.shard_map(
        shards,
        mesh=mesh,
        in_specs=(data, data, data, P(), P(), P(), P(), P(), P(), P()),
        out_specs=(data, data, data, P("ctx", "dp")),
        check_vma=False,
    )
```

time: 371 us -> 231 us (0.62)
  the two profiles are of different devices: /device:TPU:1 before, /device:TPU:16 now
where the time goes in v1:
time: 231 us
  waiting for transfers between devices  75 us (32%)
  Pallas kernels  50.7 us (22%)
  blocking collectives  49.8 us (22%)
  starting transfers between devices  32.2 us (14%)
  between operations  14.2 us (6%)
  other arithmetic  4.73 us (2%)
  local copies, waits for them, and re-layouts  4.04 us (2%)
    reduce_scatter x1, waiting for transfers between devices, shards(): mine = lax.psum_scatter(grads, 'dp', scatter_dimension=0, tiled=True)  51.6 us
    all_gather x1, blocking collectives, shards(): everyone = lax.all_gather(mine.astype(b16), 'ctx', axis=0, tiled=False)  49.8 us
    pallas_call x1, Pallas kernels, convolve(): pl.pallas_call(body, in_specs=[pl.BlockSpec(memory_space=pltpu.SMEM), vm,...  45.7 us
    all_to_all x1, starting transfers between devices, shards(): lax.all_to_all(outs, 'ctx', split_axis=0, concat_axis=0, tiled=True)  22 us
    all_to_all x1, waiting for transfers between devices, shards(): lax.all_to_all(outs, 'ctx', split_axis=0, concat_axis=0, tiled=True)  13.5 us
    all_to_all x1, starting transfers between devices, shards(): lax.all_to_all(outgoing, 'ctx', split_axis=0, concat_axis=0, tiled=True)  10.2 us
    all_to_all x1, waiting for transfers between devices, shards(): lax.all_to_all(outgoing, 'ctx', split_axis=0, concat_axis=0, tiled=True)  9.15 us
  transfers between devices with their start and end apart: 3, of which 3 were waited for; matrix products, arithmetic and copies ran while one was open for 1% of the time, Pallas kernels for 2%

profile of v1, /device:TPU:16, one launch (start us, length us, event | category | flops | bytes accessed | tf_op | source)
XLA Modules:
  0.0 230.5 jit_solution(3660650201592574189)
XLA Ops:
  7.2 1.2 fusion.3
  8.4 0.9 pad_maximum_fusion
  9.2 10.2 %all-to-all-start = ((bf16[32,64,128]{2,1,0:T(8,128)(2,1)}), bf16[32,64,128]{2,1,0:T(8,128)(2,1)S(1)}, u32[]{:S(2)}, u32[]{:S(2)}) async-start(bf16[32,64,128]{2,1,0:T(8,128)(2,1)} %pad_maximum_fusion), calls=%async_computation | async-start | bytes 1048576 | tf_op jit(solution)/shard_map/all_to_all | solution.py:270
  19.4 0.8 rsqrt_bitcast_fusion
  20.2 0.1 copy.23.refs_5_
  20.4 0.8 dynamic-slice_bitcast_fusion
  21.2 0.1 copy.22.refs_4_
  21.3 0.1 copy.24.refs_6_
  21.4 0.6 copy-done.7
  22.0 0.1 copy.20
  22.1 0.7 copy-done.2
  22.8 4.0 %taps.1.refs_2_ = f32[1056,128]{1,0:T(8,128)S(1)} custom-call(bf16[48,4096]{1,0:T(8,128)(2,1)S(1)} %copy-done.1, bf16[64,48]{1,0:T(8,128)(2,1)S(1)} %pad.4.refs_1_, bf16[64,64]{1,0:T(8,128)(2,1)S(1)} %copy-done.2, bf16[32,64]{1,0:T(8,128)(2,1)S(1)} %copy.25.refs_3_, f32[32,1]{1,0:T(8,128)S(1)} %copy.22.refs_4_, f32[32,1]{1,0:T(8,128)S(1)} %copy.23.refs_5_, ...), custom_call_target="tpu_custom_call" | custom-call | tf_op jit(solution)/shard_map/taps/pallas_call | solution.py:70
  26.9 9.2 %all-to-all-done.refs_1_ = bf16[32,64,128]{2,1,0:T(8,128)(2,1)S(1)} async-done(((bf16[32,64,128]{2,1,0:T(8,128)(2,1)}), bf16[32,64,128]{2,1,0:T(8,128)(2,1)S(1)}, u32[]{:S(2)}, u32[]{:S(2)}) %all-to-all-start) | async-done | bytes 524320 | tf_op jit(solution)/shard_map/all_to_all | solution.py:270
  36.0 45.7 %convolve.1 = (bf16[32,64,128]{2,1,0:T(8,128)(2,1)}, f32[32,32,128]{2,1,0:T(8,128)}) custom-call(s32[32]{0:T(128)S(1)} %get-tuple-element.9.refs_0_, bf16[32,64,128]{2,1,0:T(8,128)(2,1)S(1)} %all-to-all-done.refs_1_, f32[1056,128]{1,0:T(8,128)S(1)} %taps.1.refs_2_), custom_call_target="tpu_custom_call" | custom-call | tf_op jit(solution)/shard_map/convolve/pallas_call | solution.py:191
  81.7 22.0 %all-to-all-start.1 = ((bf16[32,64,128]{2,1,0:T(8,128)(2,1)}), bf16[32,64,128]{2,1,0:T(8,128)(2,1)S(1)}, u32[]{:S(2)}, u32[]{:S(2)}) async-start(bf16[32,64,128]{2,1,0:T(8,128)(2,1)} %get-tuple-element.6), calls=%async_computation.1 | async-start | bytes 1048576 | tf_op jit(solution)/shard_map/all_to_all | solution.py:286
  103.7 0.7 reduce-scatter.2.cloned.1.call-update
  104.4 13.5 %all-to-all-done.1 = bf16[32,64,128]{2,1,0:T(8,128)(2,1)S(1)} async-done(((bf16[32,64,128]{2,1,0:T(8,128)(2,1)}), bf16[32,64,128]{2,1,0:T(8,128)(2,1)S(1)}, u32[]{:S(2)}, u32[]{:S(2)}) %all-to-all-start.1) | async-done | bytes 524320 | tf_op jit(solution)/shard_map/all_to_all | solution.py:286
  118.0 0.7 copy-done.8
  118.6 1.2 fusion.1
  119.8 51.6 %reduce-scatter.2.cloned.1.call-done = f32[2,32,128]{2,1,0:T(8,128)} async-done(((f32[32,32,128]{2,1,0:T(8,128)}), f32[2,32,128]{2,1,0:T(8,128)}) %reduce-scatter.2.cloned.1.call-update) | async-done | bytes 32784 | tf_op jit(solution)/shard_map/reduce_scatter | solution.py:284
  171.5 0.8 convert_element_type.88
  172.2 49.8 %all-gather = bf16[64,32,128]{2,1,0:T(8,128)(2,1)S(1)} all-gather(bf16[2,32,128]{2,1,0:T(8,128)(2,1)S(1)} %convert_element_type.88), channel_id=2, replica_groups=mesh['dp'=16,'ctx'=32] {'ctx'}, dimensions={0}, use_global_device_ids=true | all-gather | bytes 540672 | tf_op jit(solution)/shard_map/all_gather | solution.py:285
  222.0 0.7 copy-done.3
  222.7 1.0 pick.1
  (19 shorter events, 0.3 us)
Async XLA Ops:
  7.2 13.1 %copy-start = (bf16[1024,64]{0,1:T(8,128)(2,1)S(1)}, bf16[1024,64]{0,1:T(8,128)(2,1)}, u32[]{:S(2)}) copy-start(bf16[1024,64]{0,1:T(8,128)(2,1)} %param.16) | copy-start | bytes 393220
  7.2 1.2 copy-start.6
  9.2 12.9 %copy-start.1 = (bf16[48,4096]{1,0:T(8,128)(2,1)S(1)}, bf16[48,4096]{1,0:T(8,128)(2,1)}, u32[]{:S(2)}) copy-start(bf16[48,4096]{1,0:T(8,128)(2,1)} %constant.14.clone.refs_0_) | copy-start | bytes 1179652
  9.2 26.8 %all-to-all-start = ((bf16[32,64,128]{2,1,0:T(8,128)(2,1)}), bf16[32,64,128]{2,1,0:T(8,128)(2,1)S(1)}, u32[]{:S(2)}, u32[]{:S(2)}) async-start(bf16[32,64,128]{2,1,0:T(8,128)(2,1)} %pad_maximum_fusion), calls=%async_computation | async-start | bytes 1048576 | tf_op jit(solution)/shard_map/all_to_all | solution.py:270
  21.3 0.7 copy-start.7
  22.1 0.7 copy-start.2
  81.7 36.2 %all-to-all-start.1 = ((bf16[32,64,128]{2,1,0:T(8,128)(2,1)}), bf16[32,64,128]{2,1,0:T(8,128)(2,1)S(1)}, u32[]{:S(2)}, u32[]{:S(2)}) async-start(bf16[32,64,128]{2,1,0:T(8,128)(2,1)} %get-tuple-element.6), calls=%async_computation.1 | async-start | bytes 1048576 | tf_op jit(solution)/shard_map/all_to_all | solution.py:286
  103.6 67.8 %reduce-scatter.2.cloned.1.call-start = ((), (), s32[]{:S(2)}) async-start(), calls=%async_computation.3 | async-start | bytes 557056 | tf_op jit(solution)/shard_map/reduce_scatter | solution.py:284
  104.4 13.6 %copy-start.4 = (bf16[1,1024,128]{2,1,0:T(8,128)(2,1)S(1)}, bf16[1,1024,128]{2,1,0:T(8,128)(2,1)}, u32[]{:S(2)}) copy-start(bf16[1,1024,128]{2,1,0:T(8,128)(2,1)} %param.13) | copy-start | bytes 786436
  104.4 13.6 %copy-start.5 = (bf16[1,1024,128]{2,1,0:T(8,128)(2,1)S(1)}, bf16[1,1024,128]{2,1,0:T(8,128)(2,1)}, u32[]{:S(2)}) copy-start(bf16[1,1024,128]{2,1,0:T(8,128)(2,1)} %param.12) | copy-start | bytes 786436
  118.0 0.7 copy-start.8
  222.0 0.7 copy-start.3
Sparse Core Ops, SparseCore 0:
  107.3 64.1 reduce-scatter.1

commit v2 on v1

v2 whole, which is shorter than its diff:
```python
import math

import numpy as np

import jax
import jax.numpy as jnp
import ml_dtypes
from jax import lax
from jax.experimental import pallas as pl
from jax.experimental.pallas import tpu as pltpu
from jax.sharding import PartitionSpec as P

LANES = 128
GROUP = 8
VMEM_LIMIT = 48 * 1024 * 1024
F32 = jnp.float32
B16 = jnp.bfloat16
PARAMS = pltpu.CompilerParams(vmem_limit_bytes=VMEM_LIMIT)
VM = pl.BlockSpec(memory_space=pltpu.VMEM)
SM = pl.BlockSpec(memory_space=pltpu.SMEM)


def iota(shape, axis):
    return lax.broadcasted_iota(jnp.int32, shape, axis)


def flip_matrix():
    return (iota((LANES, LANES), 0) + iota((LANES, LANES), 1) == LANES - 1).astype(F32).astype(B16)


def embed_table(seq_total, features):
    bands = (features - 1) // 2
    points = np.arange(seq_total, dtype=np.int64)
    freq_ids = np.arange(1, bands + 1, dtype=np.int64)
    phase = (freq_ids[:, None] * points[None, :] % seq_total).astype(np.float32) * np.float32(
        2.0 * math.pi / seq_total
    )
    ramp = points.astype(np.float32)[None, :] / np.float32(seq_total)
    table = np.concatenate([ramp, np.cos(phase), np.sin(phase)], axis=0)
    return table.astype(ml_dtypes.bfloat16)


def sine(x):
    turns = jnp.round(x * (1.0 / math.pi))
    r = x - turns * 3.140625
    r = r - turns * 9.67502593994140625e-4
    r = r - turns * 1.509957990978376432e-7
    half = turns * 0.5
    sign = 1.0 - 4.0 * (half - jnp.floor(half))
    s = r * r
    p = -1.0 / 39916800.0
    p = p * s + 1.0 / 362880.0
    p = p * s - 1.0 / 5040.0
    p = p * s + 1.0 / 120.0
    p = p * s - 1.0 / 6.0
    return sign * (r + r * s * p)


def pack_body(sig_ref, gate_ref, cot_ref, out_ref, wide):
    half = sig_ref.shape[0] // 2
    for part in range(2):
        rows = slice(part * half, (part + 1) * half)
        wide[pl.ds(part, half, stride=4), :] = sig_ref[rows, :].astype(F32)
        wide[pl.ds(2 + part, half, stride=4), :] = cot_ref[rows, :].astype(F32) * gate_ref[rows, :].astype(F32)
    out_ref[...] = wide[...].astype(B16)


def pack(sig, gate, cot):
    rows = 2 * sig.shape[0]
    return pl.pallas_call(
        pack_body,
        in_specs=[VM] * 3,
        out_specs=VM,
        out_shape=jax.ShapeDtypeStruct((rows, LANES), B16),
        scratch_shapes=[pltpu.VMEM((rows, LANES), F32)],
        compiler_params=PARAMS,
        name="pack",
    )(sig, gate, cot)


def tables_body(
    emb_ref, w_in_ref, w_mid_ref, w_out_ref, rate_ref, scale_ref, len_ref, ahead_ref, behind_ref, taps, turned
):
    seq_len = emb_ref.shape[1]
    width = 512
    blocks = seq_len // LANES
    channels = w_out_ref.shape[0]
    w_in = w_in_ref[...]
    w_mid = w_mid_ref[...]
    w_out = w_out_ref[...]
    flip = flip_matrix()
    zero = jnp.zeros((8, LANES), F32)
    taps[0:8, :] = zero
    turned[0:8, :] = zero
    for part in range(seq_len // width):
        emb = emb_ref[:, part * width : (part + 1) * width]
        one = sine(jnp.dot(w_in, emb, preferred_element_type=F32)).astype(B16)
        two = sine(jnp.dot(w_mid, one, preferred_element_type=F32)).astype(B16)
        net = jnp.dot(w_out, two, preferred_element_type=F32)
        point = part * width + iota((channels, width), 1)
        decay = jnp.exp(-rate_ref[...] * point.astype(F32) / seq_len)
        value = jnp.where(point < len_ref[...], net * decay * scale_ref[...], 0.0).astype(B16)
        for piece in range(width // LANES):
            block = part * (width // LANES) + piece + 1
            here = value[:, piece * LANES : (piece + 1) * LANES]
            taps[block * 8 : block * 8 + channels, :] = here.astype(F32)
            turned[block * 8 : block * 8 + channels, :] = jnp.dot(here, flip, preferred_element_type=F32)
    lane = iota((8, LANES), 1)
    sub = iota((8, LANES), 0)
    build_key = jnp.where(lane >= sub, lane, lane + LANES)

    def head(ref, row, shift):
        spread = jnp.broadcast_to(ref[row : row + 1, :], (8, LANES))
        return pltpu.roll(spread, shift, 1, stride=1, stride_axis=0)

    def fill(out_ref, spot, low, high):
        built = []
        for a in range(LANES // 8):
            piece = jnp.where(build_key >= LANES - 8 * a, low, high)
            built.append(pltpu.roll(piece, 8 * a, 1) if a else piece)
        out_ref[spot * LANES : (spot + 1) * LANES, :] = jnp.concatenate(built, axis=0).astype(B16)

    for c in range(2):
        low = head(taps, c, 0)
        back_low = head(turned, c, 1)
        for k in range(blocks):
            high = head(taps, (k + 1) * 8 + c, 0)
            back_high = head(turned, (k + 1) * 8 + c, 1)
            fill(ahead_ref, c * blocks + k, low, high)
            fill_behind(behind_ref, c * blocks + k, back_low, back_high, lane, sub)
            low = high
            back_low = back_high


def fill_behind(out_ref, spot, low, high, lane, sub):
    key = jnp.where(lane >= sub + 1, lane, lane + LANES)
    built = []
    for a in range(LANES // 8):
        piece = jnp.where(key >= LANES - 8 * a, high, low)
        built.append(pltpu.roll(piece, 8 * a, 1) if a else piece)
    out_ref[spot * LANES : (spot + 1) * LANES, :] = jnp.concatenate(built, axis=0).astype(B16)


def make_tables(emb, w_in, w_mid, w_out, rate, scale, length):
    blocks = emb.shape[1] // LANES
    shape = jax.ShapeDtypeStruct((2 * blocks * LANES, LANES), B16)
    scratch = pltpu.VMEM(((blocks + 1) * 8, LANES), F32)
    return pl.pallas_call(
        tables_body,
        in_specs=[VM] * 7,
        out_specs=(VM, VM),
        out_shape=(shape, shape),
        scratch_shapes=[scratch, scratch],
        compiler_params=PARAMS,
        name="tables",
    )(emb, w_in, w_mid, w_out, rate, scale, length)


def diagonal(upper, lower, key):
    total = None
    for a in range(LANES // 8):
        rows = slice(8 * a, 8 * a + 8)
        piece = upper[rows, :] if lower is None else lower[rows, :]
        if lower is None:
            piece = jnp.where(key >= LANES - 1 - 8 * a, piece, 0.0)
        else:
            piece = jnp.where(key >= LANES - 1 - 8 * a, upper[rows, :], piece)
        if a:
            piece = pltpu.roll(piece, 8 * a, 1)
        total = piece if total is None else total + piece
    total = pltpu.roll(total, 1, 1, stride=1, stride_axis=0)
    return jnp.sum(total, axis=0, keepdims=True)


def convolve_body(len_ref, arr_ref, ahead_ref, behind_ref, out_ref, wide, sig, back, y_acc, z_acc, lags, *, norm):
    peers = arr_ref.shape[0] // 4
    blocks = ahead_ref.shape[0] // (2 * LANES)
    batch = peers // blocks
    pad = (GROUP - 1) * batch
    flip = flip_matrix()
    key = iota((8, LANES), 0) + iota((8, LANES), 1)
    wide[0 : 4 * peers, :] = arr_ref[...].astype(F32)
    zero = jnp.zeros((pad, LANES), B16)
    lags_all = []
    for c in range(2):
        sig[c, 0:pad, :] = zero
        sig[c, pad : pad + peers, :] = wide[pl.ds(c, peers, stride=4), :].astype(B16)
        back[c, 0:peers, :] = wide[pl.ds(2 + c, peers, stride=4), :].astype(B16)
        back[c, peers : peers + pad, :] = zero
    for c in range(2):
        turned = lax.dot_general(
            flip, sig[c, pad : pad + peers, :], (((1,), (1,)), ((), ())), preferred_element_type=F32
        ).astype(B16)
        before = None
        for first in range(0, blocks, GROUP):
            rows = (blocks - first) * batch
            spots = slice((c * blocks + first) * LANES, (c * blocks + first + GROUP) * LANES)
            left = jnp.concatenate(
                [sig[c, pad - j * batch : pad - j * batch + rows, :] for j in range(GROUP)], axis=1
            )
            moved = jnp.concatenate(
                [back[c, (first + j) * batch : (first + j) * batch + rows, :] for j in range(GROUP)], axis=1
            )
            y = jnp.dot(left, ahead_ref[spots, :], preferred_element_type=F32)
            z = jnp.dot(moved, behind_ref[spots, :], preferred_element_type=F32)
            if first == 0:
                y_acc[c] = y
                z_acc[c] = z
            else:
                y_acc[c, first * batch :, :] += y
                z_acc[c, 0:rows, :] += z
            outer = jnp.dot(turned[:, 0:rows], moved, preferred_element_type=F32)
            for j in range(GROUP):
                now = outer[:, j * LANES : (j + 1) * LANES]
                if before is not None:
                    lags[c * blocks + first + j - 1 : c * blocks + first + j, :] = diagonal(before, now, key)
                before = now
        lags[c * blocks + blocks - 1 : c * blocks + blocks, :] = diagonal(before, None, key)
    point = iota((blocks, LANES), 0) * LANES + iota((blocks, LANES), 1)
    for c in range(2):
        wide[pl.ds(c, peers, stride=8), :] = y_acc[c]
        wide[pl.ds(2 + c, peers, stride=8), :] = z_acc[c]
        here = slice(c * blocks, (c + 1) * blocks)
        lags[here, :] = jnp.where(point < len_ref[c], lags[here, :] * norm, 0.0)
        for half in range(2):
            column = lags[pl.ds(c * blocks + half, batch, stride=2), :]
            wide[pl.ds(4 + 2 * c + half, peers, stride=8), :] = jnp.concatenate([column] * blocks, axis=0)
    out_ref[...] = wide[...].astype(B16)


def convolve(lengths, arrived, ahead, behind, norm):
    peers = arrived.shape[0] // 4
    blocks = ahead.shape[0] // (2 * LANES)
    pad = (GROUP - 1) * (peers // blocks)
    body = lambda *refs: convolve_body(*refs, norm=norm)
    return pl.pallas_call(
        body,
        in_specs=[SM, VM, VM, VM],
        out_specs=VM,
        out_shape=jax.ShapeDtypeStruct((8 * peers, LANES), B16),
        scratch_shapes=[
            pltpu.VMEM((8 * peers, LANES), F32),
            pltpu.VMEM((2, peers + pad, LANES), B16),
            pltpu.VMEM((2, peers + pad, LANES), B16),
            pltpu.VMEM((2, peers, LANES), F32),
            pltpu.VMEM((2, peers, LANES), F32),
            pltpu.VMEM((2 * blocks, LANES), F32),
        ],
        compiler_params=PARAMS,
        name="convolve",
    )(lengths, arrived, ahead, behind)


def finish_body(
    me_ref, ret_ref, sig_ref, gate_ref, cot_ref, skip_ref, owner_ref, result_ref, d_gate_ref, d_sig_ref, grad_ref, wide
):
    wide[...] = ret_ref[...].astype(F32)
    half = sig_ref.shape[0] // 2
    for part in range(2):
        rows = slice(part * half, (part + 1) * half)
        skip = skip_ref[rows, :]
        gate = gate_ref[rows, :].astype(F32)
        cot = cot_ref[rows, :].astype(F32)
        mixed = wide[pl.ds(part, half, stride=8), :] + skip * sig_ref[rows, :].astype(F32)
        result_ref[rows, :] = (gate * mixed).astype(B16)
        d_gate_ref[rows, :] = (cot * mixed).astype(B16)
        d_sig_ref[rows, :] = (skip * (cot * gate) + wide[pl.ds(2 + part, half, stride=8), :]).astype(B16)
    mine = (owner_ref[...] == me_ref[0]).astype(F32)
    lines = mine.shape[0]
    above = (iota((LANES, LANES), 0) < iota((LANES, LANES), 1)).astype(F32).astype(B16)
    within = jnp.dot(mine.astype(B16), above, preferred_element_type=F32)
    counts = jnp.sum(mine, axis=1, keepdims=True)
    slots = grad_ref.shape[0]
    slot_id = iota((slots, LANES), 0).astype(F32)
    start = jnp.zeros((1, 1), F32)
    pieces = []
    for line in range(lines):
        rank = within[line : line + 1, :] + start
        hit = jnp.where(slot_id == rank, mine[line : line + 1, :], 0.0)
        pieces.append(hit.astype(B16))
        start = start + counts[line : line + 1, :]
    chosen = jnp.concatenate(pieces, axis=1)
    for column in range(2):
        table = jnp.concatenate(
            [wide[pl.ds(4 + 2 * c + column, half, stride=8), :].astype(B16) for c in range(2)], axis=0
        )
        grad_ref[:, column * LANES : (column + 1) * LANES] = jnp.dot(chosen, table, preferred_element_type=F32)


def finish(me, returned, sig, gate, cot, skip, owner, slots):
    data = jax.ShapeDtypeStruct(sig.shape, B16)
    return pl.pallas_call(
        finish_body,
        in_specs=[SM] + [VM] * 6,
        out_specs=(VM,) * 4,
        out_shape=(data, data, data, jax.ShapeDtypeStruct((slots, 2 * LANES), F32)),
        scratch_shapes=[pltpu.VMEM(returned.shape, F32)],
        compiler_params=PARAMS,
        name="finish",
    )(me, returned, sig, gate, cot, skip[:, None], owner.reshape(-1, LANES))


def exchange(array):
    return lax.all_to_all(array, ("ctx", "dp"), split_axis=0, concat_axis=0, tiled=True)


def shards(signal, gate, cotangent, w_in, w_mid, w_out, rates, skip, lengths, owner):
    ctx_count = lax.axis_size("ctx")
    dp_count = lax.axis_size("dp")
    ctx_place = lax.axis_index("ctx")
    channels, local_len = signal.shape[1:]
    seq_len = local_len * ctx_count
    norm = 1.0 / math.sqrt(seq_len * dp_count)
    peers = ctx_count * dp_count
    place = ctx_place * dp_count + lax.axis_index("dp")

    sig, gat, cot = signal[0], gate[0], cotangent[0]
    packed = pack(sig, gat, cot)
    arrived = exchange(packed)

    def own(array):
        return lax.dynamic_slice_in_dim(array.reshape(2, peers, -1), place, 1, 1)[:, 0]

    def wide_rows(array):
        return jnp.pad(array, ((0, 6), (0, 0)))

    features = w_in.shape[1]
    padded = -(-features // 16) * 16
    table = np.zeros((padded, seq_len), ml_dtypes.bfloat16)
    table[:features] = embed_table(seq_len, features)
    w_in_wide = jnp.pad(w_in, ((0, 0), (0, padded - features)))
    own_lengths = own(lengths)
    ahead, behind = make_tables(
        jnp.asarray(table),
        w_in_wide,
        w_mid,
        wide_rows(own(w_out)),
        wide_rows(own(rates)),
        wide_rows(lax.rsqrt(own_lengths.astype(F32))),
        wide_rows(own_lengths),
    )
    outs = convolve(own_lengths[:, 0], arrived, ahead, behind, norm)
    returned = exchange(outs)
    result, d_gate, d_signal, tap_grad = finish(
        ctx_place.reshape(1).astype(jnp.int32), returned, sig, gat, cot, skip, owner, 2 * channels // ctx_count
    )
    return (result[None], d_gate[None], d_signal[None], tap_grad)


def solution(mesh):
    data = P("dp", None, "ctx")
    return jax.shard_map(
        shards,
        mesh=mesh,
        in_specs=(data, data, data, P(), P(), P(), P(), P(), P(), P()),
        out_specs=(data, data, data, P("ctx", "dp")),
        check_vma=False,
    )
```

time: 231 us -> 99.5 us (0.43)
  the two profiles are of different devices: /device:TPU:16 before, /device:TPU:1 now
where the time goes in v2:
time: 99.5 us; the launch traced here: 99.2 us
  waiting for transfers between devices  45 us (45%)
  starting transfers between devices  31.1 us (31%)
  Pallas kernels  15.4 us (15%)
  local copies, waits for them, and re-layouts  6.74 us (7%)
    all_to_all x2, waiting for transfers between devices, exchange(): lax.all_to_all(array, ('ctx', 'dp'), split_axis=0, concat_axis=0, tiled=T...  45 us
    all_to_all x2, starting transfers between devices, exchange(): lax.all_to_all(array, ('ctx', 'dp'), split_axis=0, concat_axis=0, tiled=T...  31.1 us
    pallas_call x1, Pallas kernels, make_tables(): pl.pallas_call(tables_body, in_specs=[VM] * 7, out_specs=(VM, VM), out_sh...  6.86 us
    pallas_call x1, Pallas kernels, convolve(): pl.pallas_call(body, in_specs=[SM, VM, VM, VM], out_specs=VM, out_shape=j...  6.04 us
    unnamed x34, local copies, waits for them, and re-layouts  6.01 us
  transfers between devices with their start and end apart: 2, of which 2 were waited for; matrix products, arithmetic and copies ran while one was open for 1% of the time, Pallas kernels for 7%

profile of v2, /device:TPU:1, one launch (start us, length us, event | category | flops | bytes accessed | tf_op | source)
XLA Modules:
  0.0 99.2 jit_solution(4918439186399285504)
XLA Ops:
  0.6 0.0 copy-start.14
  0.6 0.0 copy-start.2
  0.7 0.9 copy-done.2
  1.6 0.9 copy-done.4
  2.6 0.9 copy-done.6
  3.5 1.0 %pack.1 = bf16[2048,128]{1,0:T(8,128)(2,1)} custom-call(bf16[1024,128]{1,0:T(8,128)(2,1)S(1)} %bitcast.23, bf16[1024,128]{1,0:T(8,128)(2,1)S(1)} %bitcast.25, bf16[1024,128]{1,0:T(8,128)(2,1)S(1)} %bitcast.27), custom_call_target="tpu_custom_call" | custom-call | tf_op jit(solution)/shard_map/pack/pallas_call | solution.py:70
  4.5 22.2 %all-to-all-start = ((bf16[512,4,128]{2,1,0:T(4,128)(2,1)}), bf16[512,4,128]{2,1,0:T(4,128)(2,1)S(1)}, u32[]{:S(2)}, u32[]{:S(2)}) async-start(bf16[512,4,128]{2,1,0:T(4,128)(2,1)} %bitcast.4), calls=%async_computation | async-start | bytes 1048576 | tf_op jit(solution)/shard_map/all_to_all | solution.py:304
  26.7 0.2 fusion.1.refs_0_
  26.9 0.1 convert_rsqrt_fusion
  27.0 0.1 reshape.45
  27.1 0.1 constant_dynamic-slice_fusion
  27.2 0.1 copy.32
  27.3 0.1 dynamic-slice_bitcast_fusion
  27.4 0.1 copy.26
  27.6 6.9 %tables.1 = (bf16[8192,128]{1,0:T(8,128)(2,1)S(1)}, bf16[8192,128]{1,0:T(8,128)(2,1)S(1)}) custom-call(bf16[48,4096]{1,0:T(8,128)(2,1)S(1)} %copy-done.8, bf16[64,48]{1,0:T(8,128)(2,1)S(1)} %pad.19.w_in_ref, bf16[64,64]{1,0:T(8,128)(2,1)S(1)} %copy-done.9, bf16[8,64]{1,0:T(8,128)(2,1)S(1)} %pad.20.w_out_ref, f32[8,1]{1,0:T(8,128)S(1)} %pad.21.rate_ref, ...), custom_call_target="tpu_custom_call" | custom-call | tf_op jit(solution)/shard_map/tables/pallas_call | solution.py:148
  34.4 1.3 %copy-done = bf16[8192,128]{1,0:T(8,128)(2,1)} copy-done((bf16[8192,128]{1,0:T(8,128)(2,1)}, bf16[8192,128]{1,0:T(8,128)(2,1)S(1)}, u32[]{:S(2)}) %copy-start) | copy-done | bytes 2097176
  35.8 12.8 %all-to-all-done = bf16[512,4,128]{2,1,0:T(4,128)(2,1)S(1)} async-done(((bf16[512,4,128]{2,1,0:T(4,128)(2,1)}), bf16[512,4,128]{2,1,0:T(4,128)(2,1)S(1)}, u32[]{:S(2)}, u32[]{:S(2)}) %all-to-all-start) | async-done | bytes 524320 | tf_op jit(solution)/shard_map/all_to_all | solution.py:304
  48.5 1.6 %copy-done.1 = bf16[8192,128]{1,0:T(8,128)(2,1)S(1)} copy-done((bf16[8192,128]{1,0:T(8,128)(2,1)S(1)}, bf16[8192,128]{1,0:T(8,128)(2,1)}, u32[]{:S(2)}) %copy-start.1) | copy-done | bytes 2097176
  50.1 6.0 %convolve.1 = bf16[4096,128]{1,0:T(8,128)(2,1)} custom-call(s32[2]{0:T(128)S(1)} %fusion.1.refs_0_, bf16[2048,128]{1,0:T(8,128)(2,1)S(1)} %bitcast.22, bf16[8192,128]{1,0:T(8,128)(2,1)S(1)} %get-tuple-element.10.refs_2_, bf16[8192,128]{1,0:T(8,128)(2,1)S(1)} %copy-done.1), custom_call_target="tpu_custom_call" | custom-call | tf_op jit(solution)/shard_map/convolve/pallas_call | solution.py:236
  56.2 0.0 copy-start.10
  56.2 9.0 %all-to-all-start.1 = ((bf16[512,8,128]{2,1,0:T(8,128)(2,1)}), bf16[512,8,128]{2,1,0:T(8,128)(2,1)S(1)}, u32[]{:S(2)}, u32[]{:S(2)}) async-start(bf16[512,8,128]{2,1,0:T(8,128)(2,1)} %bitcast.9), calls=%async_computation.1 | async-start | bytes 2097152 | tf_op jit(solution)/shard_map/all_to_all | solution.py:304
  65.2 0.2 copy.31.skip_ref
  65.4 32.2 %all-to-all-done.1 = bf16[512,8,128]{2,1,0:T(8,128)(2,1)S(1)} async-done(((bf16[512,8,128]{2,1,0:T(8,128)(2,1)}), bf16[512,8,128]{2,1,0:T(8,128)(2,1)S(1)}, u32[]{:S(2)}, u32[]{:S(2)}) %all-to-all-start.1) | async-done | bytes 1048608 | tf_op jit(solution)/shard_map/all_to_all | solution.py:304
  97.7 1.5 %finish.1 = (bf16[1024,128]{1,0:T(8,128)(2,1)}, bf16[1024,128]{1,0:T(8,128)(2,1)}, bf16[1024,128]{1,0:T(8,128)(2,1)}, f32[64,256]{1,0:T(8,128)}) custom-call(s32[1]{0:T(128)} %bitcast.me_ref, bf16[4096,128]{1,0:T(8,128)(2,1)S(1)} %bitcast.21, bf16[1024,128]{1,0:T(8,128)(2,1)S(1)} %bitcast.24, bf16[1024,128]{1,0:T(8,128)(2,1)S(1)} %bitcast.26, ...), custom_call_target="tpu_custom_call" | custom-call | tf_op jit(solution)/shard_map/finish/pallas_call | solution.py:292
  (31 shorter events, 0.1 us)
Async XLA Ops:
  0.6 26.1 %copy-start.14 = (s32[1024]{0:T(1024)S(1)}, s32[1024]{0:T(1024)}, u32[]{:S(2)}) copy-start(s32[1024]{0:T(1024)} %param.19) | copy-start | bytes 12292
  0.6 1.0 copy-start.2
  1.6 0.9 copy-start.4
  2.5 0.9 copy-start.6
  3.5 23.5 %copy-start.11 = (bf16[1024,64]{0,1:T(8,128)(2,1)S(1)}, bf16[1024,64]{0,1:T(8,128)(2,1)}, u32[]{:S(2)}) copy-start(bf16[1024,64]{0,1:T(8,128)(2,1)} %param.16) | copy-start | bytes 393220
  3.5 23.8 %copy-start.15 = (f32[1024]{0:T(1024)S(1)}, f32[1024]{0:T(1024)}, u32[]{:S(2)}) copy-start(f32[1024]{0:T(1024)} %param.17) | copy-start | bytes 12292
  3.5 23.9 %copy-start.12 = (bf16[64,33]{0,1:T(8,128)(2,1)S(1)}, bf16[64,33]{0,1:T(8,128)(2,1)}, u32[]{:S(2)}) copy-start(bf16[64,33]{0,1:T(8,128)(2,1)} %param.14) | copy-start | bytes 12676
  3.5 24.0 %copy-start.8 = (bf16[48,4096]{1,0:T(8,128)(2,1)S(1)}, bf16[48,4096]{1,0:T(8,128)(2,1)}, u32[]{:S(2)}) copy-start(bf16[48,4096]{1,0:T(8,128)(2,1)} %constant.21.clone.emb_ref) | copy-start | bytes 1179652
  3.5 24.0 %copy-start.9 = (bf16[64,64]{1,0:T(8,128)(2,1)S(1)}, bf16[64,64]{1,0:T(8,128)(2,1)}, u32[]{:S(2)}) copy-start(bf16[64,64]{1,0:T(8,128)(2,1)} %w_mid_ref.1) | copy-start | bytes 24580
  4.5 44.0 %all-to-all-start = ((bf16[512,4,128]{2,1,0:T(4,128)(2,1)}), bf16[512,4,128]{2,1,0:T(4,128)(2,1)S(1)}, u32[]{:S(2)}, u32[]{:S(2)}) async-start(bf16[512,4,128]{2,1,0:T(4,128)(2,1)} %bitcast.4), calls=%async_computation | async-start | bytes 1048576 | tf_op jit(solution)/shard_map/all_to_all | solution.py:304
  34.4 1.3 %copy-start = (bf16[8192,128]{1,0:T(8,128)(2,1)}, bf16[8192,128]{1,0:T(8,128)(2,1)S(1)}, u32[]{:S(2)}) copy-start(bf16[8192,128]{1,0:T(8,128)(2,1)S(1)} %get-tuple-element.11.refs_3_) | copy-start | bytes 6291460
  48.5 1.6 %copy-start.1 = (bf16[8192,128]{1,0:T(8,128)(2,1)S(1)}, bf16[8192,128]{1,0:T(8,128)(2,1)}, u32[]{:S(2)}) copy-start(bf16[8192,128]{1,0:T(8,128)(2,1)} %copy-done) | copy-start | bytes 6291460
  56.2 9.0 %copy-start.13 = (f32[1024]{0:T(1024)S(1)}, f32[1024]{0:T(1024)}, u32[]{:S(2)}) copy-start(f32[1024]{0:T(1024)} %param.18) | copy-start | bytes 12292
  56.2 41.5 %copy-start.3 = (bf16[1,1024,128]{2,1,0:T(8,128)(2,1)S(1)}, bf16[1,1024,128]{2,1,0:T(8,128)(2,1)}, u32[]{:S(2)}) copy-start(bf16[1,1024,128]{2,1,0:T(8,128)(2,1)} %param.11) | copy-start | bytes 786436
  56.2 41.5 %copy-start.5 = (bf16[1,1024,128]{2,1,0:T(8,128)(2,1)S(1)}, bf16[1,1024,128]{2,1,0:T(8,128)(2,1)}, u32[]{:S(2)}) copy-start(bf16[1,1024,128]{2,1,0:T(8,128)(2,1)} %param.12) | copy-start | bytes 786436
  56.2 41.5 %copy-start.7 = (bf16[1,1024,128]{2,1,0:T(8,128)(2,1)S(1)}, bf16[1,1024,128]{2,1,0:T(8,128)(2,1)}, u32[]{:S(2)}) copy-start(bf16[1,1024,128]{2,1,0:T(8,128)(2,1)} %param.13) | copy-start | bytes 786436
  56.2 41.5 %copy-start.10 = (s32[1024]{0:T(1024)S(1)}, s32[1024]{0:T(1024)}, u32[]{:S(2)}) copy-start(s32[1024]{0:T(1024)} %param.20) | copy-start | bytes 12292
  56.2 41.4 %all-to-all-start.1 = ((bf16[512,8,128]{2,1,0:T(8,128)(2,1)}), bf16[512,8,128]{2,1,0:T(8,128)(2,1)S(1)}, u32[]{:S(2)}, u32[]{:S(2)}) async-start(bf16[512,8,128]{2,1,0:T(8,128)(2,1)} %bitcast.9), calls=%async_computation.1 | async-start | bytes 2097152 | tf_op jit(solution)/shard_map/all_to_all | solution.py:304

commit v3 on v2

--- a/solution.py
+++ b/solution.py
@@ -12,12 +12,14 @@
 
 LANES = 128
 GROUP = 8
-VMEM_LIMIT = 48 * 1024 * 1024
+PACK_PARTS = 4
+VMEM_LIMIT = 16 * 1024 * 1024
 F32 = jnp.float32
 B16 = jnp.bfloat16
 PARAMS = pltpu.CompilerParams(vmem_limit_bytes=VMEM_LIMIT)
 VM = pl.BlockSpec(memory_space=pltpu.VMEM)
 SM = pl.BlockSpec(memory_space=pltpu.SMEM)
+HB = pl.BlockSpec(memory_space=pltpu.HBM)
 
 
 def iota(shape, axis):
@@ -56,30 +58,67 @@
     return sign * (r + r * s * p)
 
 
-def pack_body(sig_ref, gate_ref, cot_ref, out_ref, wide):
-    half = sig_ref.shape[0] // 2
-    for part in range(2):
-        rows = slice(part * half, (part + 1) * half)
-        wide[pl.ds(part, half, stride=4), :] = sig_ref[rows, :].astype(F32)
-        wide[pl.ds(2 + part, half, stride=4), :] = cot_ref[rows, :].astype(F32) * gate_ref[rows, :].astype(F32)
-    out_ref[...] = wide[...].astype(B16)
+def pack_body(sig_hbm, gate_hbm, cot_hbm, out_hbm, sig_in, gate_in, cot_in, wide, out, in_sem, out_sem):
+    half = sig_in.shape[0] // 2
+    step = half // PACK_PARTS
+    pairs = ((sig_hbm, sig_in), (gate_hbm, gate_in), (cot_hbm, cot_in))
+
+    def reads(part):
+        copies = []
+        for which, (src, dst) in enumerate(pairs):
+            for side in range(2):
+                rows = pl.ds(side * half + part * step, step)
+                sem = in_sem.at[(part * 3 + which) * 2 + side]
+                copies.append(pltpu.make_async_copy(src.at[rows, :], dst.at[rows, :], sem))
+        return copies
+
+    def write(part):
+        rows = pl.ds(part * 4 * step, 4 * step)
+        return pltpu.make_async_copy(out.at[rows, :], out_hbm.at[rows, :], out_sem.at[part])
+
+    for part in range(PACK_PARTS):
+        for copy in reads(part):
+            copy.start()
+    for part in range(PACK_PARTS):
+        for copy in reads(part):
+            copy.wait()
+        for side in range(2):
+            rows = slice(side * half + part * step, side * half + (part + 1) * step)
+            first = part * 4 * step
+            back = cot_in[rows, :].astype(F32) * gate_in[rows, :].astype(F32)
+            wide[pl.ds(first + side, step, stride=4), :] = sig_in[rows, :].astype(F32)
+            wide[pl.ds(first + 2 + side, step, stride=4), :] = back
+        rows = slice(part * 4 * step, (part + 1) * 4 * step)
+        out[rows, :] = wide[rows, :].astype(B16)
+        write(part).start()
+    for part in range(PACK_PARTS):
+        write(part).wait()
 
 
 def pack(sig, gate, cot):
     rows = 2 * sig.shape[0]
+    held = pltpu.VMEM(sig.shape, B16)
     return pl.pallas_call(
         pack_body,
-        in_specs=[VM] * 3,
-        out_specs=VM,
+        in_specs=[HB] * 3,
+        out_specs=HB,
         out_shape=jax.ShapeDtypeStruct((rows, LANES), B16),
-        scratch_shapes=[pltpu.VMEM((rows, LANES), F32)],
+        scratch_shapes=[
+            held,
+            held,
+            held,
+            pltpu.VMEM((rows, LANES), F32),
+            pltpu.VMEM((rows, LANES), B16),
+            pltpu.SemaphoreType.DMA((6 * PACK_PARTS,)),
+            pltpu.SemaphoreType.DMA((PACK_PARTS,)),
+        ],
         compiler_params=PARAMS,
         name="pack",
-    )(sig, gate, cot)
+    )(*(pltpu.with_memory_space_constraint(array, pltpu.HBM) for array in (sig, gate, cot)))
 
 
 def tables_body(
-    emb_ref, w_in_ref, w_mid_ref, w_out_ref, rate_ref, scale_ref, len_ref, ahead_ref, behind_ref, taps, turned
+    emb_ref, w_in_ref, w_mid_ref, w_out_ref, rate_ref, scale_ref, len_ref, ahead_ref, taps
 ):
     seq_len = emb_ref.shape[1]
     width = 512
@@ -88,10 +127,7 @@
     w_in = w_in_ref[...]
     w_mid = w_mid_ref[...]
     w_out = w_out_ref[...]
-    flip = flip_matrix()
-    zero = jnp.zeros((8, LANES), F32)
-    taps[0:8, :] = zero
-    turned[0:8, :] = zero
+    taps[0:8, :] = jnp.zeros((8, LANES), F32)
     for part in range(seq_len // width):
         emb = emb_ref[:, part * width : (part + 1) * width]
         one = sine(jnp.dot(w_in, emb, preferred_element_type=F32)).astype(B16)
@@ -104,41 +140,27 @@
             block = part * (width // LANES) + piece + 1
             here = value[:, piece * LANES : (piece + 1) * LANES]
             taps[block * 8 : block * 8 + channels, :] = here.astype(F32)
-            turned[block * 8 : block * 8 + channels, :] = jnp.dot(here, flip, preferred_element_type=F32)
     lane = iota((8, LANES), 1)
     sub = iota((8, LANES), 0)
     build_key = jnp.where(lane >= sub, lane, lane + LANES)
 
-    def head(ref, row, shift):
-        spread = jnp.broadcast_to(ref[row : row + 1, :], (8, LANES))
-        return pltpu.roll(spread, shift, 1, stride=1, stride_axis=0)
-
-    def fill(out_ref, spot, low, high):
+    def head(row):
+        spread = jnp.broadcast_to(taps[row : row + 1, :], (8, LANES))
+        return pltpu.roll(spread, 0, 1, stride=1, stride_axis=0)
+
+    def fill(spot, low, high):
         built = []
         for a in range(LANES // 8):
             piece = jnp.where(build_key >= LANES - 8 * a, low, high)
             built.append(pltpu.roll(piece, 8 * a, 1) if a else piece)
-        out_ref[spot * LANES : (spot + 1) * LANES, :] = jnp.concatenate(built, axis=0).astype(B16)
+        ahead_ref[spot * LANES : (spot + 1) * LANES, :] = jnp.concatenate(built, axis=0).astype(B16)
 
     for c in range(2):
-        low = head(taps, c, 0)
-        back_low = head(turned, c, 1)
+        low = head(0)
         for k in range(blocks):
-            high = head(taps, (k + 1) * 8 + c, 0)
-            back_high = head(turned, (k + 1) * 8 + c, 1)
-            fill(ahead_ref, c * blocks + k, low, high)
-            fill_behind(behind_ref, c * blocks + k, back_low, back_high, lane, sub)
+            high = head((k + 1) * 8 + c)
+            fill(c * blocks + k, low, high)
             low = high
-            back_low = back_high
-
-
-def fill_behind(out_ref, spot, low, high, lane, sub):
-    key = jnp.where(lane >= sub + 1, lane, lane + LANES)
-    built = []
-    for a in range(LANES // 8):
-        piece = jnp.where(key >= LANES - 8 * a, high, low)
-        built.append(pltpu.roll(piece, 8 * a, 1) if a else piece)
-    out_ref[spot * LANES : (spot + 1) * LANES, :] = jnp.concatenate(built, axis=0).astype(B16)
 
 
 def make_tables(emb, w_in, w_mid, w_out, rate, scale, length):
@@ -148,9 +170,9 @@
     return pl.pallas_call(
         tables_body,
         in_specs=[VM] * 7,
-        out_specs=(VM, VM),
-        out_shape=(shape, shape),
-        scratch_shapes=[scratch, scratch],
+        out_specs=VM,
+        out_shape=shape,
+        scratch_shapes=[scratch],
         compiler_params=PARAMS,
         name="tables",
     )(emb, w_in, w_mid, w_out, rate, scale, length)
@@ -172,7 +194,7 @@
     return jnp.sum(total, axis=0, keepdims=True)
 
 
-def convolve_body(len_ref, arr_ref, ahead_ref, behind_ref, out_ref, wide, sig, back, y_acc, z_acc, lags, *, norm):
+def convolve_body(len_ref, arr_ref, ahead_ref, out_ref, wide, sig, back, y_acc, z_acc, lags, *, norm):
     peers = arr_ref.shape[0] // 4
     blocks = ahead_ref.shape[0] // (2 * LANES)
     batch = peers // blocks
@@ -202,7 +224,10 @@
                 [back[c, (first + j) * batch : (first + j) * batch + rows, :] for j in range(GROUP)], axis=1
             )
             y = jnp.dot(left, ahead_ref[spots, :], preferred_element_type=F32)
-            z = jnp.dot(moved, behind_ref[spots, :], preferred_element_type=F32)
+            table = jnp.concatenate(
+                [ahead_ref[spots.start + j * LANES : spots.start + (j + 1) * LANES, :] for j in range(GROUP)], axis=1
+            )
+            z = lax.dot_general(moved, table, (((1,), (1,)), ((), ())), preferred_element_type=F32)
             if first == 0:
                 y_acc[c] = y
                 z_acc[c] = z
@@ -228,14 +253,14 @@
     out_ref[...] = wide[...].astype(B16)
 
 
-def convolve(lengths, arrived, ahead, behind, norm):
+def convolve(lengths, arrived, ahead, norm):
     peers = arrived.shape[0] // 4
     blocks = ahead.shape[0] // (2 * LANES)
     pad = (GROUP - 1) * (peers // blocks)
     body = lambda *refs: convolve_body(*refs, norm=norm)
     return pl.pallas_call(
         body,
-        in_specs=[SM, VM, VM, VM],
+        in_specs=[SM, VM, VM],
         out_specs=VM,
         out_shape=jax.ShapeDtypeStruct((8 * peers, LANES), B16),
         scratch_shapes=[
@@ -248,7 +273,7 @@
         ],
         compiler_params=PARAMS,
         name="convolve",
-    )(lengths, arrived, ahead, behind)
+    )(lengths, arrived, ahead)
 
 
 def finish_body(
@@ -330,7 +355,7 @@
     table[:features] = embed_table(seq_len, features)
     w_in_wide = jnp.pad(w_in, ((0, 0), (0, padded - features)))
     own_lengths = own(lengths)
-    ahead, behind = make_tables(
+    ahead = make_tables(
         jnp.asarray(table),
         w_in_wide,
         w_mid,
@@ -339,7 +364,7 @@
         wide_rows(lax.rsqrt(own_lengths.astype(F32))),
         wide_rows(own_lengths),
     )
-    outs = convolve(own_lengths[:, 0], arrived, ahead, behind, norm)
+    outs = convolve(own_lengths[:, 0], arrived, ahead, norm)
     returned = exchange(outs)
     result, d_gate, d_signal, tap_grad = finish(
         ctx_place.reshape(1).astype(jnp.int32), returned, sig, gat, cot, skip, owner, 2 * channels // ctx_count

time: 99.5 us -> 96 us (0.965)
  local copies, waits for them, and re-layouts: 6.74 us -> 0.97 us
  waiting for transfers between devices: 45 us -> 47.8 us
    unnamed x34 -> x24, local copies, waits for them, and re-layouts: 6.01 us -> 0.25 us
    all_to_all x2, waiting for transfers between devices: 45 us -> 47.8 us  [exchange(): lax.all_to_all(array, ('ctx', 'dp'), split_axis=0, concat_axis=0, tiled=T...]
  transfers between devices with their start and end apart: 2 -> 2, of which waited for: 2 -> 2; matrix products, arithmetic and copies ran while one was open for 1% -> 1% of each run, Pallas kernels for 7% -> 6%
where the time goes in v3:
time: 96 us; the launch traced here: 95.8 us
  waiting for transfers between devices  47.8 us (50%)
  starting transfers between devices  31.1 us (32%)
  Pallas kernels  15 us (16%)
  local copies, waits for them, and re-layouts  0.97 us (1%)
    all_to_all x2, waiting for transfers between devices, exchange(): lax.all_to_all(array, ('ctx', 'dp'), split_axis=0, concat_axis=0, tiled=T...  47.8 us
    all_to_all x2, starting transfers between devices, exchange(): lax.all_to_all(array, ('ctx', 'dp'), split_axis=0, concat_axis=0, tiled=T...  31.1 us
    pallas_call x1, Pallas kernels, convolve(): pl.pallas_call(body, in_specs=[SM, VM, VM], out_specs=VM, out_shape=jax.S...  5.99 us
    pallas_call x1, Pallas kernels, make_tables(): pl.pallas_call(tables_body, in_specs=[VM] * 7, out_specs=VM, out_shape=sh...  5.41 us
    pallas_call x1, Pallas kernels, pack(): pl.pallas_call(pack_body, in_specs=[HB] * 3, out_specs=HB, out_shape=jax....  2.08 us
  transfers between devices with their start and end apart: 2, of which 2 were waited for; matrix products, arithmetic and copies ran while one was open for 1% of the time, Pallas kernels for 6%

profile of v3, /device:TPU:1, one launch (start us, length us, event | category | flops | bytes accessed | tf_op | source)
XLA Modules:
  0.0 95.8 jit_solution(15677239262494828037)
XLA Ops:
  0.6 0.0 copy-start.3
  0.6 0.0 copy-start.9
  0.7 0.0 copy-start.6
  0.7 0.0 copy-start.10
  0.7 0.0 copy-start.7
  0.7 0.0 copy-start.4
  0.7 2.1 %pack.1 = bf16[2048,128]{1,0:T(8,128)(2,1)} custom-call(bf16[1024,128]{1,0:T(8,128)(2,1)} %bitcast.23, bf16[1024,128]{1,0:T(8,128)(2,1)} %bitcast.25, bf16[1024,128]{1,0:T(8,128)(2,1)} %bitcast.27), custom_call_target="tpu_custom_call" | custom-call | tf_op jit(solution)/shard_map/pack/pallas_call | solution.py:101
  2.8 22.2 %all-to-all-start = ((bf16[512,4,128]{2,1,0:T(4,128)(2,1)}), bf16[512,4,128]{2,1,0:T(4,128)(2,1)S(1)}, u32[]{:S(2)}, u32[]{:S(2)}) async-start(bf16[512,4,128]{2,1,0:T(4,128)(2,1)} %bitcast.4), calls=%async_computation | async-start | bytes 1048576 | tf_op jit(solution)/shard_map/all_to_all | solution.py:329
  25.0 0.0 copy-done.9
  25.0 0.2 fusion.1.refs_0_
  25.2 0.1 convert_rsqrt_fusion
  25.3 0.1 reshape.45
  25.4 0.1 constant_dynamic-slice_fusion
  25.5 0.1 copy.32
  25.6 0.1 dynamic-slice_bitcast_fusion
  25.7 0.1 copy.26
  25.8 5.4 %tables.1.refs_2_ = bf16[8192,128]{1,0:T(8,128)(2,1)S(1)} custom-call(bf16[48,4096]{1,0:T(8,128)(2,1)S(1)} %copy-done.3, bf16[64,48]{1,0:T(8,128)(2,1)S(1)} %pad.19.w_in_ref, bf16[64,64]{1,0:T(8,128)(2,1)S(1)} %copy-done.4, bf16[8,64]{1,0:T(8,128)(2,1)S(1)} %pad.20.w_out_ref, f32[8,1]{1,0:T(8,128)S(1)} %pad.21.rate_ref, f32[8,1]{1,0:T(8,128)S(1)} %pad.22.scale_ref, ...), custom_call_target="tpu_custom_call" | custom-call | tf_op jit(solution)/shard_map/tables/pallas_call | solution.py:170
  31.2 15.6 %all-to-all-done = bf16[512,4,128]{2,1,0:T(4,128)(2,1)S(1)} async-done(((bf16[512,4,128]{2,1,0:T(4,128)(2,1)}), bf16[512,4,128]{2,1,0:T(4,128)(2,1)S(1)}, u32[]{:S(2)}, u32[]{:S(2)}) %all-to-all-start) | async-done | bytes 524320 | tf_op jit(solution)/shard_map/all_to_all | solution.py:329
  46.8 6.0 %convolve.1 = bf16[4096,128]{1,0:T(8,128)(2,1)} custom-call(s32[2]{0:T(128)S(1)} %fusion.1.refs_0_, bf16[2048,128]{1,0:T(8,128)(2,1)S(1)} %bitcast.22, bf16[8192,128]{1,0:T(8,128)(2,1)S(1)} %tables.1.refs_2_), custom_call_target="tpu_custom_call" | custom-call | tf_op jit(solution)/shard_map/convolve/pallas_call | solution.py:261
  52.8 8.9 %all-to-all-start.1 = ((bf16[512,8,128]{2,1,0:T(8,128)(2,1)}), bf16[512,8,128]{2,1,0:T(8,128)(2,1)S(1)}, u32[]{:S(2)}, u32[]{:S(2)}) async-start(bf16[512,8,128]{2,1,0:T(8,128)(2,1)} %bitcast.9), calls=%async_computation.1 | async-start | bytes 2097152 | tf_op jit(solution)/shard_map/all_to_all | solution.py:329
  61.8 0.2 copy.31.skip_ref
  62.0 32.2 %all-to-all-done.1 = bf16[512,8,128]{2,1,0:T(8,128)(2,1)S(1)} async-done(((bf16[512,8,128]{2,1,0:T(8,128)(2,1)}), bf16[512,8,128]{2,1,0:T(8,128)(2,1)S(1)}, u32[]{:S(2)}, u32[]{:S(2)}) %all-to-all-start.1) | async-done | bytes 1048608 | tf_op jit(solution)/shard_map/all_to_all | solution.py:329
  94.2 0.0 copy-done.1
  94.3 1.5 %finish.1 = (bf16[1024,128]{1,0:T(8,128)(2,1)}, bf16[1024,128]{1,0:T(8,128)(2,1)}, bf16[1024,128]{1,0:T(8,128)(2,1)}, f32[64,256]{1,0:T(8,128)}) custom-call(s32[1]{0:T(128)} %bitcast.me_ref, bf16[4096,128]{1,0:T(8,128)(2,1)S(1)} %bitcast.21, bf16[1024,128]{1,0:T(8,128)(2,1)S(1)} %bitcast.24, bf16[1024,128]{1,0:T(8,128)(2,1)S(1)} %bitcast.26, ...), custom_call_target="tpu_custom_call" | custom-call | tf_op jit(solution)/shard_map/finish/pallas_call | solution.py:317
  (21 shorter events, 0.1 us)
Async XLA Ops:
  0.6 25.2 %copy-start.3 = (bf16[48,4096]{1,0:T(8,128)(2,1)S(1)}, bf16[48,4096]{1,0:T(8,128)(2,1)}, u32[]{:S(2)}) copy-start(bf16[48,4096]{1,0:T(8,128)(2,1)} %constant.21.clone.emb_ref) | copy-start | bytes 1179652
  0.6 24.3 %copy-start.9 = (s32[1024]{0:T(1024)S(1)}, s32[1024]{0:T(1024)}, u32[]{:S(2)}) copy-start(s32[1024]{0:T(1024)} %param.19) | copy-start | bytes 12292
  0.7 24.6 %copy-start.6 = (bf16[1024,64]{0,1:T(8,128)(2,1)S(1)}, bf16[1024,64]{0,1:T(8,128)(2,1)}, u32[]{:S(2)}) copy-start(bf16[1024,64]{0,1:T(8,128)(2,1)} %param.16) | copy-start | bytes 393220
  0.7 24.9 %copy-start.10 = (f32[1024]{0:T(1024)S(1)}, f32[1024]{0:T(1024)}, u32[]{:S(2)}) copy-start(f32[1024]{0:T(1024)} %param.17) | copy-start | bytes 12292
  0.7 25.0 %copy-start.7 = (bf16[64,33]{0,1:T(8,128)(2,1)S(1)}, bf16[64,33]{0,1:T(8,128)(2,1)}, u32[]{:S(2)}) copy-start(bf16[64,33]{0,1:T(8,128)(2,1)} %param.14) | copy-start | bytes 12676
  0.7 25.1 %copy-start.4 = (bf16[64,64]{1,0:T(8,128)(2,1)S(1)}, bf16[64,64]{1,0:T(8,128)(2,1)}, u32[]{:S(2)}) copy-start(bf16[64,64]{1,0:T(8,128)(2,1)} %w_mid_ref.1) | copy-start | bytes 24580
  2.8 44.0 %all-to-all-start = ((bf16[512,4,128]{2,1,0:T(4,128)(2,1)}), bf16[512,4,128]{2,1,0:T(4,128)(2,1)S(1)}, u32[]{:S(2)}, u32[]{:S(2)}) async-start(bf16[512,4,128]{2,1,0:T(4,128)(2,1)} %bitcast.4), calls=%async_computation | async-start | bytes 1048576 | tf_op jit(solution)/shard_map/all_to_all | solution.py:329
  46.8 15.0 %copy-start.8 = (f32[1024]{0:T(1024)S(1)}, f32[1024]{0:T(1024)}, u32[]{:S(2)}) copy-start(f32[1024]{0:T(1024)} %param.18) | copy-start | bytes 12292
  52.8 41.4 %copy-start = (bf16[1,1024,128]{2,1,0:T(8,128)(2,1)S(1)}, bf16[1,1024,128]{2,1,0:T(8,128)(2,1)}, u32[]{:S(2)}) copy-start(bf16[1,1024,128]{2,1,0:T(8,128)(2,1)} %param.11) | copy-start | bytes 786436
  52.8 41.4 %copy-start.1 = (bf16[1,1024,128]{2,1,0:T(8,128)(2,1)S(1)}, bf16[1,1024,128]{2,1,0:T(8,128)(2,1)}, u32[]{:S(2)}) copy-start(bf16[1,1024,128]{2,1,0:T(8,128)(2,1)} %param.12) | copy-start | bytes 786436
  52.8 41.4 %copy-start.2 = (bf16[1,1024,128]{2,1,0:T(8,128)(2,1)S(1)}, bf16[1,1024,128]{2,1,0:T(8,128)(2,1)}, u32[]{:S(2)}) copy-start(bf16[1,1024,128]{2,1,0:T(8,128)(2,1)} %param.13) | copy-start | bytes 786436
  52.8 41.4 %copy-start.5 = (s32[1024]{0:T(1024)S(1)}, s32[1024]{0:T(1024)}, u32[]{:S(2)}) copy-start(s32[1024]{0:T(1024)} %param.20) | copy-start | bytes 12292
  52.8 41.4 %all-to-all-start.1 = ((bf16[512,8,128]{2,1,0:T(8,128)(2,1)}), bf16[512,8,128]{2,1,0:T(8,128)(2,1)S(1)}, u32[]{:S(2)}, u32[]{:S(2)}) async-start(bf16[512,8,128]{2,1,0:T(8,128)(2,1)} %bitcast.9), calls=%async_computation.1 | async-start | bytes 2097152 | tf_op jit(solution)/shard_map/all_to_all | solution.py:329

commit v4 on v3

v4 whole, which is shorter than its diff:
```python
import math

import numpy as np

import jax
import jax.numpy as jnp
import ml_dtypes
from jax import lax
from jax.experimental import pallas as pl
from jax.experimental.pallas import tpu as pltpu
from jax.sharding import PartitionSpec as P

LANES = 128
GROUP = 8
PACK_PARTS = 4
VMEM_LIMIT = 16 * 1024 * 1024
F32 = jnp.float32
B16 = jnp.bfloat16
PARAMS = pltpu.CompilerParams(vmem_limit_bytes=VMEM_LIMIT)
VM = pl.BlockSpec(memory_space=pltpu.VMEM)
SM = pl.BlockSpec(memory_space=pltpu.SMEM)
HB = pl.BlockSpec(memory_space=pltpu.HBM)


def far(*arrays):
    return [pltpu.with_memory_space_constraint(array, pltpu.HBM) for array in arrays]


def iota(shape, axis):
    return lax.broadcasted_iota(jnp.int32, shape, axis)


def flip_matrix():
    return (iota((LANES, LANES), 0) + iota((LANES, LANES), 1) == LANES - 1).astype(F32).astype(B16)


def embed_table(seq_total, features):
    bands = (features - 1) // 2
    points = np.arange(seq_total, dtype=np.int64)
    freq_ids = np.arange(1, bands + 1, dtype=np.int64)
    phase = (freq_ids[:, None] * points[None, :] % seq_total).astype(np.float32) * np.float32(
        2.0 * math.pi / seq_total
    )
    ramp = points.astype(np.float32)[None, :] / np.float32(seq_total)
    table = np.concatenate([ramp, np.cos(phase), np.sin(phase)], axis=0)
    return table.astype(ml_dtypes.bfloat16)


def sine(x):
    turns = jnp.round(x * (1.0 / math.pi))
    r = x - turns * 3.140625
    r = r - turns * 9.67502593994140625e-4
    r = r - turns * 1.509957990978376432e-7
    half = turns * 0.5
    sign = 1.0 - 4.0 * (half - jnp.floor(half))
    s = r * r
    p = -1.0 / 39916800.0
    p = p * s + 1.0 / 362880.0
    p = p * s - 1.0 / 5040.0
    p = p * s + 1.0 / 120.0
    p = p * s - 1.0 / 6.0
    return sign * (r + r * s * p)


def owner_order(owner, holders):
    above = (iota((LANES, LANES), 0) < iota((LANES, LANES), 1)).astype(F32).astype(B16)
    before = (iota((holders, holders), 1) < iota((holders, holders), 0)).astype(F32).astype(B16)
    holder = iota((holders, LANES), 0)
    marks = []
    ahead = []
    seen = jnp.zeros((holders, 1), F32)
    for line in range(owner.shape[0]):
        mark = (holder == owner[line : line + 1, :]).astype(F32)
        marks.append(mark)
        ahead.append(jnp.dot(mark.astype(B16), above, preferred_element_type=F32) + seen)
        seen = seen + jnp.sum(mark, axis=1, keepdims=True)
    total = jnp.broadcast_to(seen, (holders, LANES)).astype(B16)
    start = jnp.dot(before, total, preferred_element_type=F32)
    return [jnp.sum(m * (a + start), axis=0, keepdims=True) for m, a in zip(marks, ahead)]


def pack_body(
    owner_hbm, sig_hbm, gate_hbm, cot_hbm, out_hbm, spot_ref,
    owner_in, sig_in, gate_in, cot_in, wide, out, owner_sem, in_sem, out_sem, *, holders
):
    channels = sig_in.shape[0]
    half = channels // 2
    step = channels // PACK_PARTS
    pairs = ((sig_hbm, sig_in), (gate_hbm, gate_in), (cot_hbm, cot_in))

    def reads(part):
        rows = pl.ds(part * step, step)
        return [
            pltpu.make_async_copy(src.at[rows, :], dst.at[rows, :], in_sem.at[part * 3 + which])
            for which, (src, dst) in enumerate(pairs)
        ]

    def write(part):
        rows = pl.ds(part * 2 * step, 2 * step)
        return pltpu.make_async_copy(out.at[rows, :], out_hbm.at[rows, :], out_sem.at[part])

    owner_copy = pltpu.make_async_copy(owner_hbm, owner_in, owner_sem.at[0])
    owner_copy.start()
    for part in range(PACK_PARTS):
        for copy in reads(part):
            copy.start()
    owner_copy.wait()
    spots = owner_order(owner_in[...], holders)
    place = iota((channels, LANES), 0).astype(F32)
    lines = [jnp.where(place == spot, 1.0, 0.0).astype(B16) for spot in spots]
    for line, spot in enumerate(spots):
        spot_ref[line : line + 1, :] = spot
    spot_ref[len(spots) :, :] = owner_in[...].astype(F32)
    values = []
    for part in range(PACK_PARTS):
        for copy in reads(part):
            copy.wait()
        rows = slice(part * step, (part + 1) * step)
        back = (cot_in[rows, :].astype(F32) * gate_in[rows, :].astype(F32)).astype(B16)
        values.append(jnp.concatenate([sig_in[rows, :], back], axis=1))
    moved = jnp.dot(
        jnp.concatenate(lines, axis=1), jnp.concatenate(values, axis=0), preferred_element_type=F32
    )
    for side in range(2):
        rows = slice(side * half, (side + 1) * half)
        wide[pl.ds(side, half, stride=4), :] = moved[rows, 0:LANES]
        wide[pl.ds(2 + side, half, stride=4), :] = moved[rows, LANES:]
    for part in range(PACK_PARTS):
        rows = slice(part * 2 * step, (part + 1) * 2 * step)
        out[rows, :] = wide[rows, :].astype(B16)
        write(part).start()
    for part in range(PACK_PARTS):
        write(part).wait()


def pack(owner, sig, gate, cot, holders):
    rows = 2 * sig.shape[0]
    held = pltpu.VMEM(sig.shape, B16)
    lines = owner.shape[0]
    return pl.pallas_call(
        lambda *refs: pack_body(*refs, holders=holders),
        in_specs=[HB] * 4,
        out_specs=(HB, VM),
        out_shape=(jax.ShapeDtypeStruct((rows, LANES), B16), jax.ShapeDtypeStruct((2 * lines, LANES), F32)),
        scratch_shapes=[
            pltpu.VMEM(owner.shape, jnp.int32),
            held,
            held,
            held,
            pltpu.VMEM((rows, LANES), F32),
            pltpu.VMEM((rows, LANES), B16),
            pltpu.SemaphoreType.DMA((1,)),
            pltpu.SemaphoreType.DMA((3 * PACK_PARTS,)),
            pltpu.SemaphoreType.DMA((PACK_PARTS,)),
        ],
        compiler_params=PARAMS,
        name="pack",
    )(*far(owner, sig, gate, cot))


def tables_body(
    place_ref, emb_hbm, w_in_ref, w_mid_hbm, w_out_hbm, rate_hbm, len_hbm, spot_ref, ahead_ref, own_ref,
    emb_ref, w_mid_ref, w_out_ref, rate_ref, len_ref, taps, in_sem
):
    seq_len = emb_ref.shape[1]
    width = 512
    blocks = seq_len // LANES
    channels = w_out_ref.shape[1]
    lines = channels // LANES
    pairs = (
        (rate_hbm, rate_ref), (len_hbm, len_ref), (w_out_hbm, w_out_ref), (w_mid_hbm, w_mid_ref), (emb_hbm, emb_ref)
    )
    copies = [pltpu.make_async_copy(src, dst, in_sem.at[which]) for which, (src, dst) in enumerate(pairs)]
    for copy in copies:
        copy.start()
    for copy in copies:
        copy.wait()
    target = (iota((8, LANES), 0) * (channels // 2) + place_ref[0]).astype(F32)
    marks = [jnp.where(spot_ref[line : line + 1, :] == target, 1.0, 0.0) for line in range(lines)]

    def chosen(ref, first=0):
        total = 0.0
        for line in range(lines):
            total = total + marks[line] * ref[first + line : first + line + 1, :].astype(F32)
        return jnp.sum(total, axis=1, keepdims=True)

    rate = chosen(rate_ref)
    length = chosen(len_ref)
    own_ref[0:2, :] = jnp.broadcast_to(length[0:2, :], (2, LANES))
    own_ref[2:4, :] = jnp.broadcast_to(chosen(spot_ref, lines)[0:2, :], (2, LANES))
    own_ref[4:8, :] = jnp.zeros((4, LANES), F32)
    scale = lax.rsqrt(jnp.maximum(length, 1.0))
    w_in = w_in_ref[...]
    w_mid = w_mid_ref[...]
    w_out = lax.dot_general(
        jnp.concatenate(marks, axis=1).astype(B16), w_out_ref[...], (((1,), (1,)), ((), ())), preferred_element_type=F32
    ).astype(B16)
    taps[0:8, :] = jnp.zeros((8, LANES), F32)
    for part in range(seq_len // width):
        emb = emb_ref[:, part * width : (part + 1) * width]
        one = sine(jnp.dot(w_in, emb, preferred_element_type=F32)).astype(B16)
        two = sine(jnp.dot(w_mid, one, preferred_element_type=F32)).astype(B16)
        net = jnp.dot(w_out, two, preferred_element_type=F32)
        point = (part * width + iota((8, width), 1)).astype(F32)
        decay = jnp.exp(-rate * point / seq_len)
        value = jnp.where(point < length, net * decay * scale, 0.0).astype(B16)
        for piece in range(width // LANES):
            block = part * (width // LANES) + piece + 1
            here = value[:, piece * LANES : (piece + 1) * LANES]
            taps[block * 8 : block * 8 + 8, :] = here.astype(F32)
    lane = iota((8, LANES), 1)
    sub = iota((8, LANES), 0)
    build_key = jnp.where(lane >= sub, lane, lane + LANES)

    def head(row):
        spread = jnp.broadcast_to(taps[row : row + 1, :], (8, LANES))
        return pltpu.roll(spread, 0, 1, stride=1, stride_axis=0)

    def fill(spot, low, high):
        built = []
        for a in range(LANES // 8):
            piece = jnp.where(build_key >= LANES - 8 * a, low, high)
            built.append(pltpu.roll(piece, 8 * a, 1) if a else piece)
        ahead_ref[spot * LANES : (spot + 1) * LANES, :] = jnp.concatenate(built, axis=0).astype(B16)

    for c in range(2):
        low = head(0)
        for k in range(blocks):
            high = head((k + 1) * 8 + c)
            fill(c * blocks + k, low, high)
            low = high


def make_tables(place, emb, w_in, w_mid, w_out, rate, length, spots):
    blocks = emb.shape[1] // LANES
    rate = rate.reshape(-1, LANES)
    length = length.reshape(-1, LANES)
    w_out = w_out.T
    held = [pltpu.VMEM(array.shape, array.dtype) for array in (emb, w_mid, w_out, rate, length)]
    emb, w_mid, w_out, rate, length = far(emb, w_mid, w_out, rate, length)
    return pl.pallas_call(
        tables_body,
        in_specs=[SM, HB, VM, HB, HB, HB, HB, VM],
        out_specs=(VM, VM),
        out_shape=(
            jax.ShapeDtypeStruct((2 * blocks * LANES, LANES), B16),
            jax.ShapeDtypeStruct((8, LANES), F32),
        ),
        scratch_shapes=[*held, pltpu.VMEM(((blocks + 1) * 8, LANES), F32), pltpu.SemaphoreType.DMA((5,))],
        compiler_params=PARAMS,
        name="tables",
    )(place, emb, w_in, w_mid, w_out, rate, length, spots)


def diagonal(upper, lower, key):
    total = None
    for a in range(LANES // 8):
        rows = slice(8 * a, 8 * a + 8)
        piece = upper[rows, :] if lower is None else lower[rows, :]
        if lower is None:
            piece = jnp.where(key >= LANES - 1 - 8 * a, piece, 0.0)
        else:
            piece = jnp.where(key >= LANES - 1 - 8 * a, upper[rows, :], piece)
        if a:
            piece = pltpu.roll(piece, 8 * a, 1)
        total = piece if total is None else total + piece
    total = pltpu.roll(total, 1, 1, stride=1, stride_axis=0)
    return jnp.sum(total, axis=0, keepdims=True)


def convolve_body(
    own_ref, arr_ref, ahead_ref, out_hbm, done_ref, wide, sig, back, y_acc, z_acc, lags, out, out_sem, *, norm
):
    peers = arr_ref.shape[0] // 4
    blocks = ahead_ref.shape[0] // (2 * LANES)
    batch = peers // blocks
    pad = (GROUP - 1) * batch
    flip = flip_matrix()
    key = iota((8, LANES), 0) + iota((8, LANES), 1)
    wide[0 : 4 * peers, :] = arr_ref[...].astype(F32)
    zero = jnp.zeros((pad, LANES), B16)
    for c in range(2):
        sig[c, 0:pad, :] = zero
        sig[c, pad : pad + peers, :] = wide[pl.ds(c, peers, stride=4), :].astype(B16)
        back[c, 0:peers, :] = wide[pl.ds(2 + c, peers, stride=4), :].astype(B16)
        back[c, peers : peers + pad, :] = zero
    for c in range(2):
        turned = lax.dot_general(
            flip, sig[c, pad : pad + peers, :], (((1,), (1,)), ((), ())), preferred_element_type=F32
        ).astype(B16)
        before = None
        for first in range(0, blocks, GROUP):
            rows = (blocks - first) * batch
            spots = slice((c * blocks + first) * LANES, (c * blocks + first + GROUP) * LANES)
            left = jnp.concatenate(
                [sig[c, pad - j * batch : pad - j * batch + rows, :] for j in range(GROUP)], axis=1
            )
            moved = jnp.concatenate(
                [back[c, (first + j) * batch : (first + j) * batch + rows, :] for j in range(GROUP)], axis=1
            )
            y = jnp.dot(left, ahead_ref[spots, :], preferred_element_type=F32)
            table = jnp.concatenate(
                [ahead_ref[spots.start + j * LANES : spots.start + (j + 1) * LANES, :] for j in range(GROUP)], axis=1
            )
            z = lax.dot_general(moved, table, (((1,), (1,)), ((), ())), preferred_element_type=F32)
            if first == 0:
                y_acc[c] = y
                z_acc[c] = z
            else:
                y_acc[c, first * batch :, :] += y
                z_acc[c, 0:rows, :] += z
            outer = jnp.dot(turned[:, 0:rows], moved, preferred_element_type=F32)
            for j in range(GROUP):
                now = outer[:, j * LANES : (j + 1) * LANES]
                if before is not None:
                    lags[c * blocks + first + j - 1 : c * blocks + first + j, :] = diagonal(before, now, key)
                before = now
        lags[c * blocks + blocks - 1 : c * blocks + blocks, :] = diagonal(before, None, key)
    point = (iota((blocks, LANES), 0) * LANES + iota((blocks, LANES), 1)).astype(F32)
    holder = jnp.concatenate([jnp.full((batch, LANES), h, jnp.int32) for h in range(blocks)], axis=0).astype(F32)
    for c in range(2):
        wide[pl.ds(c, peers, stride=6), :] = y_acc[c]
        wide[pl.ds(2 + c, peers, stride=6), :] = z_acc[c]
        here = slice(c * blocks, (c + 1) * blocks)
        lags[here, :] = jnp.where(point < own_ref[c : c + 1, :], lags[here, :] * norm, 0.0)
    for half in range(2):
        total = jnp.zeros((peers, LANES), F32)
        for c in range(2):
            column = lags[pl.ds(c * blocks + half, batch, stride=2), :]
            column = jnp.concatenate([column] * blocks, axis=0)
            total = jnp.where(holder == own_ref[2 + c : 3 + c, :], column, total)
        wide[pl.ds(4 + half, peers, stride=6), :] = total
    step = 6 * peers // PACK_PARTS

    def write(part):
        rows = pl.ds(part * step, step)
        return pltpu.make_async_copy(out.at[rows, :], out_hbm.at[rows, :], out_sem.at[part])

    for part in range(PACK_PARTS):
        rows = slice(part * step, (part + 1) * step)
        out[rows, :] = wide[rows, :].astype(B16)
        write(part).start()
    done_ref[...] = own_ref[...]
    for part in range(PACK_PARTS):
        write(part).wait()


def convolve(own, arrived, ahead, norm):
    peers = arrived.shape[0] // 4
    blocks = ahead.shape[0] // (2 * LANES)
    pad = (GROUP - 1) * (peers // blocks)
    body = lambda *refs: convolve_body(*refs, norm=norm)
    return pl.pallas_call(
        body,
        in_specs=[VM, VM, VM],
        out_specs=(HB, VM),
        out_shape=(jax.ShapeDtypeStruct((6 * peers, LANES), B16), jax.ShapeDtypeStruct(own.shape, F32)),
        scratch_shapes=[
            pltpu.VMEM((6 * peers, LANES), F32),
            pltpu.VMEM((2, peers + pad, LANES), B16),
            pltpu.VMEM((2, peers + pad, LANES), B16),
            pltpu.VMEM((2, peers, LANES), F32),
            pltpu.VMEM((2, peers, LANES), F32),
            pltpu.VMEM((2 * blocks, LANES), F32),
            pltpu.VMEM((6 * peers, LANES), B16),
            pltpu.SemaphoreType.DMA((PACK_PARTS,)),
        ],
        compiler_params=PARAMS,
        name="convolve",
    )(own, arrived, ahead)


def route_body(
    after_ref, spot_ref, skip_ref, sig_hbm, gate_hbm, cot_hbm, out_ref, direct_ref, pulled_ref, gate_ref, cot_ref, sig_ref, in_sem
):
    pairs = ((sig_hbm, sig_ref), (gate_hbm, gate_ref), (cot_hbm, cot_ref))
    copies = [pltpu.make_async_copy(src, dst, in_sem.at[which]) for which, (src, dst) in enumerate(pairs)]
    for copy in copies:
        copy.start()

    def turned(ref, line):
        return jnp.broadcast_to(ref[line : line + 1, :], (LANES, LANES)).T

    for line in range(skip_ref.shape[0]):
        out_ref[line * LANES : (line + 1) * LANES, :] = turned(spot_ref, line)
    for copy in copies:
        copy.wait()
    for line in range(skip_ref.shape[0]):
        rows = slice(line * LANES, (line + 1) * LANES)
        skip = turned(skip_ref, line)
        direct_ref[rows, :] = skip * sig_ref[rows, :].astype(F32)
        pulled_ref[rows, :] = skip * (cot_ref[rows, :].astype(F32) * gate_ref[rows, :].astype(F32))


def route(after, spots, skip, sig, gate, cot):
    data = jax.ShapeDtypeStruct(sig.shape, B16)
    wide = jax.ShapeDtypeStruct(sig.shape, F32)
    return pl.pallas_call(
        route_body,
        in_specs=[VM] * 3 + [HB] * 3,
        out_specs=(VM,) * 5,
        out_shape=(wide, wide, wide, data, data),
        scratch_shapes=[pltpu.VMEM(sig.shape, B16), pltpu.SemaphoreType.DMA((3,))],
        compiler_params=PARAMS,
        name="route",
    )(after, spots, skip.reshape(-1, LANES), *far(sig, gate, cot))


def finish_body(
    me_ref, ret_ref, route_ref, direct_ref, pulled_ref, gate_ref, cot_ref, spot_ref,
    result_hbm, d_gate_hbm, d_sig_hbm, grad_ref, wide, result, d_gate, d_sig, out_sem
):
    wide[...] = ret_ref[...].astype(F32)
    channels = gate_ref.shape[0]
    half = channels // 2

    def take(row):
        return wide[pl.ds(row, half, stride=6), :].astype(B16)

    sides = [jnp.concatenate([take(c), take(2 + c)], axis=1) for c in range(2)]
    arrived = jnp.concatenate(sides, axis=0)
    step = channels // PACK_PARTS
    pairs = ((result, result_hbm), (d_gate, d_gate_hbm), (d_sig, d_sig_hbm))

    def writes(part):
        rows = pl.ds(part * step, step)
        return [
            pltpu.make_async_copy(src.at[rows, :], dst.at[rows, :], out_sem.at[part * 3 + which])
            for which, (src, dst) in enumerate(pairs)
        ]

    lane = iota((step, LANES), 1).astype(F32)
    for part in range(PACK_PARTS):
        rows = slice(part * step, (part + 1) * step)
        spot = route_ref[rows, :]
        lines = [jnp.where(lane + line * LANES == spot, 1.0, 0.0).astype(B16) for line in range(channels // LANES)]
        both = jnp.dot(jnp.concatenate(lines, axis=1), arrived, preferred_element_type=F32)
        mixed = both[:, 0:LANES] + direct_ref[rows, :]
        result[rows, :] = (gate_ref[rows, :].astype(F32) * mixed).astype(B16)
        d_gate[rows, :] = (cot_ref[rows, :].astype(F32) * mixed).astype(B16)
        d_sig[rows, :] = (pulled_ref[rows, :] + both[:, LANES:]).astype(B16)
        for copy in writes(part):
            copy.start()

    def tally(hits):
        lanes = jnp.sum(hits.astype(F32), axis=0, keepdims=True)
        return jnp.sum(lanes, axis=1, keepdims=True)

    slots = grad_ref.shape[0]
    owner = spot_ref[spot_ref.shape[0] // 2 :, :]
    me = me_ref[0].astype(F32)
    slot = iota((slots, half), 0).astype(F32)
    first = tally(owner < me)
    count = tally(owner == me)
    source = slot + first
    source = jnp.where(source >= half, source - half, source)
    chosen = jnp.where((iota((slots, half), 1).astype(F32) == source) & (slot < count), 1.0, 0.0).astype(B16)
    table = jnp.concatenate([take(4), take(5)], axis=1)
    grad_ref[...] = jnp.dot(chosen, table, preferred_element_type=F32)
    for part in range(PACK_PARTS):
        for copy in writes(part):
            copy.wait()


def finish(me, returned, routed, spots, slots):
    gate = routed[3]
    data = jax.ShapeDtypeStruct(gate.shape, B16)
    held = pltpu.VMEM(gate.shape, B16)
    return pl.pallas_call(
        finish_body,
        in_specs=[SM] + [VM] * 7,
        out_specs=(HB, HB, HB, VM),
        out_shape=(data, data, data, jax.ShapeDtypeStruct((slots, 2 * LANES), F32)),
        scratch_shapes=[
            pltpu.VMEM(returned.shape, F32),
            held,
            held,
            held,
            pltpu.SemaphoreType.DMA((3 * PACK_PARTS,)),
        ],
        compiler_params=PARAMS,
        name="finish",
    )(me, returned, *routed, spots)


def exchange(array, rows):
    parts = lax.all_to_all(
        array.reshape(-1, rows, LANES), ("ctx", "dp"), split_axis=0, concat_axis=0, tiled=True
    )
    return parts.reshape(array.shape)


def shards(signal, gate, cotangent, w_in, w_mid, w_out, rates, skip, lengths, owner):
    ctx_count = lax.axis_size("ctx")
    dp_count = lax.axis_size("dp")
    ctx_place = lax.axis_index("ctx")
    channels, local_len = signal.shape[1:]
    seq_len = local_len * ctx_count
    norm = 1.0 / math.sqrt(seq_len * dp_count)
    place = ctx_place * dp_count + lax.axis_index("dp")

    sig, gat, cot = signal[0], gate[0], cotangent[0]
    owner = owner.reshape(-1, LANES)
    packed, spots = pack(owner, sig, gat, cot, ctx_count)
    arrived = exchange(packed, 4)

    features = w_in.shape[1]
    padded = -(-features // 16) * 16
    table = np.zeros((padded, seq_len), ml_dtypes.bfloat16)
    table[:features] = embed_table(seq_len, features)
    w_in_wide = jnp.pad(w_in, ((0, 0), (0, padded - features)))
    ahead, own = make_tables(
        place.reshape(1).astype(jnp.int32), jnp.asarray(table), w_in_wide, w_mid, w_out, rates, lengths, spots
    )
    outs, done = convolve(own, arrived, ahead, norm)
    routed = route(done, spots, skip, sig, gat, cot)
    returned = exchange(outs, 2)
    result, d_gate, d_signal, tap_grad = finish(
        ctx_place.reshape(1).astype(jnp.int32), returned, routed, spots, 2 * channels // ctx_count
    )
    return (result[None], d_gate[None], d_signal[None], tap_grad)


def solution(mesh):
    data = P("dp", None, "ctx")
    return jax.shard_map(
        shards,
        mesh=mesh,
        in_specs=(data, data, data, P(), P(), P(), P(), P(), P(), P()),
        out_specs=(data, data, data, P("ctx", "dp")),
        check_vma=False,
    )
```

time: 96 us -> 91.5 us (0.953)
  waiting for transfers between devices: 47.8 us -> 40.6 us
  Pallas kernels: 15 us -> 17.9 us
    all_to_all x2, waiting for transfers between devices: 47.8 us -> 40.6 us  [exchange(): lax.all_to_all(array.reshape(-1, rows, LANES), ('ctx', 'dp'), split_axis=...]
    pallas_call x4 -> x5, Pallas kernels: 15 us -> 17.9 us  [the longest x1 6.21 us: make_tables(): pl.pallas_call(tables_body, in_specs=[SM, HB, VM, HB, HB, HB, HB, VM], ou...]
  transfers between devices with their start and end apart: 2 -> 2, of which waited for: 2 -> 2; matrix products, arithmetic and copies ran while one was open for 1% -> 1% of each run, Pallas kernels for 6% -> 8%
where the time goes in v4:
time: 91.5 us; the launch traced here: 91.2 us
  waiting for transfers between devices  40.6 us (44%)
  starting transfers between devices  31 us (34%)
  Pallas kernels  17.9 us (20%)
    all_to_all x2, waiting for transfers between devices, exchange(): lax.all_to_all(array.reshape(-1, rows, LANES), ('ctx', 'dp'), split_axis=...  40.6 us
    all_to_all x2, starting transfers between devices, exchange(): lax.all_to_all(array.reshape(-1, rows, LANES), ('ctx', 'dp'), split_axis=...  31 us
    pallas_call x1, Pallas kernels, make_tables(): pl.pallas_call(tables_body, in_specs=[SM, HB, VM, HB, HB, HB, HB, VM], ou...  6.21 us
    pallas_call x1, Pallas kernels, convolve(): pl.pallas_call(body, in_specs=[VM, VM, VM], out_specs=(HB, VM), out_shape...  5.11 us
    pallas_call x1, Pallas kernels, pack(): pl.pallas_call(lambda *refs: pack_body(*refs, holders=holders), in_specs=...  2.94 us
    pallas_call x1, Pallas kernels, finish(): pl.pallas_call(finish_body, in_specs=[SM] + [VM] * 7, out_specs=(HB, HB,...  2.33 us
  transfers between devices with their start and end apart: 2, of which 2 were waited for; matrix products, arithmetic and copies ran while one was open for 1% of the time, Pallas kernels for 8%

profile of v4, /device:TPU:1, one launch (start us, length us, event | category | flops | bytes accessed | tf_op | source)
XLA Modules:
  0.0 91.2 jit_solution(6891210287464525752)
XLA Ops:
  0.6 2.9 %pack.1 = (bf16[2048,128]{1,0:T(8,128)(2,1)}, f32[16,128]{1,0:T(8,128)S(1)}) custom-call(s32[8,128]{1,0:T(8,128)} %bitcast.27, bf16[1024,128]{1,0:T(8,128)(2,1)} %bitcast.20, bf16[1024,128]{1,0:T(8,128)(2,1)} %bitcast.22, bf16[1024,128]{1,0:T(8,128)(2,1)} %bitcast.24), custom_call_target="tpu_custom_call" | custom-call | tf_op jit(solution)/shard_map/pack/pallas_call | solution.py:140
  3.6 22.2 %all-to-all-start = ((bf16[512,4,128]{2,1,0:T(4,128)(2,1)}), bf16[512,4,128]{2,1,0:T(4,128)(2,1)S(1)}, u32[]{:S(2)}, u32[]{:S(2)}) async-start(bf16[512,4,128]{2,1,0:T(4,128)(2,1)} %bitcast.9), calls=%async_computation | async-start | bytes 1048576 | tf_op jit(solution)/shard_map/all_to_all | solution.py:487
  25.8 0.8 copy.15
  26.6 6.2 %tables.1 = (bf16[8192,128]{1,0:T(8,128)(2,1)S(1)}, f32[8,128]{1,0:T(8,128)S(1)}) custom-call(s32[1]{0:T(128)} %bitcast.1.place_ref, bf16[48,4096]{1,0:T(8,128)(2,1)} %constant.16.clone.emb_hbm, bf16[64,48]{1,0:T(8,128)(2,1)S(1)} %pad.4.w_in_ref, bf16[64,64]{1,0:T(8,128)(2,1)} %w_mid_hbm.1, bf16[64,1024]{1,0:T(8,128)(2,1)} %bitcast.26, f32[8,128]{1,0:T(8,128)} %bitcast.28, ...), custom_call_target="tpu_custom_call" | custom-call | tf_op jit(solution)/shard_map/tables/pallas_call | solution.py:241
  32.8 14.8 %all-to-all-done = bf16[512,4,128]{2,1,0:T(4,128)(2,1)S(1)} async-done(((bf16[512,4,128]{2,1,0:T(4,128)(2,1)}), bf16[512,4,128]{2,1,0:T(4,128)(2,1)S(1)}, u32[]{:S(2)}, u32[]{:S(2)}) %all-to-all-start) | async-done | bytes 524320 | tf_op jit(solution)/shard_map/all_to_all | solution.py:487
  47.6 0.0 copy-start
  47.6 5.1 %convolve.1 = (bf16[3072,128]{1,0:T(8,128)(2,1)}, f32[8,128]{1,0:T(8,128)S(1)}) custom-call(f32[8,128]{1,0:T(8,128)S(1)} %get-tuple-element.20.refs_0_, bf16[2048,128]{1,0:T(8,128)(2,1)S(1)} %bitcast.18, bf16[8192,128]{1,0:T(8,128)(2,1)S(1)} %get-tuple-element.22.refs_2_), custom_call_target="tpu_custom_call" | custom-call | tf_op jit(solution)/shard_map/convolve/pallas_call | solution.py:353
  52.7 8.8 %all-to-all-start.1 = ((bf16[1536,2,128]{2,1,0:T(2,128)(2,1)}), bf16[1536,2,128]{2,1,0:T(2,128)(2,1)S(1)}, u32[]{:S(2)}, u32[]{:S(2)}) async-start(bf16[1536,2,128]{2,1,0:T(2,128)(2,1)} %bitcast.11), calls=%async_computation.1 | async-start | bytes 1572864 | tf_op jit(solution)/shard_map/all_to_all | solution.py:487
  61.6 0.0 copy-done
  61.6 1.3 %route.1 = (f32[1024,128]{1,0:T(8,128)S(1)}, f32[1024,128]{1,0:T(8,128)S(1)}, f32[1024,128]{1,0:T(8,128)S(1)}, bf16[1024,128]{1,0:T(8,128)(2,1)S(1)}, bf16[1024,128]{1,0:T(8,128)(2,1)S(1)}) custom-call(f32[8,128]{1,0:T(8,128)S(1)} %get-tuple-element.24.after_ref, f32[16,128]{1,0:T(8,128)S(1)} %get-tuple-element.19.spot_ref, f32[8,128]{1,0:T(8,128)S(1)} %bitcast.19, ...), custom_call_target="tpu_custom_call" | custom-call | tf_op jit(solution)/shard_map/route/pallas_call | solution.py:398
  62.9 25.8 %all-to-all-done.1 = bf16[1536,2,128]{2,1,0:T(2,128)(2,1)S(1)} async-done(((bf16[1536,2,128]{2,1,0:T(2,128)(2,1)}), bf16[1536,2,128]{2,1,0:T(2,128)(2,1)S(1)}, u32[]{:S(2)}, u32[]{:S(2)}) %all-to-all-start.1) | async-done | bytes 786464 | tf_op jit(solution)/shard_map/all_to_all | solution.py:487
  88.7 2.3 %finish.1 = (bf16[1024,128]{1,0:T(8,128)(2,1)}, bf16[1024,128]{1,0:T(8,128)(2,1)}, bf16[1024,128]{1,0:T(8,128)(2,1)}, f32[64,256]{1,0:T(8,128)}) custom-call(s32[1]{0:T(128)} %bitcast.me_ref, bf16[3072,128]{1,0:T(8,128)(2,1)S(1)} %bitcast.17, f32[1024,128]{1,0:T(8,128)S(1)} %get-tuple-element.25.route_ref, f32[1024,128]{1,0:T(8,128)S(1)} %get-tuple-element.26.direct_ref, ...), custom_call_target="tpu_custom_call" | custom-call | tf_op jit(solution)/shard_map/finish/pallas_call | solution.py:469
  (1 shorter events, 0.0 us)
Async XLA Ops:
  3.6 44.0 %all-to-all-start = ((bf16[512,4,128]{2,1,0:T(4,128)(2,1)}), bf16[512,4,128]{2,1,0:T(4,128)(2,1)S(1)}, u32[]{:S(2)}, u32[]{:S(2)}) async-start(bf16[512,4,128]{2,1,0:T(4,128)(2,1)} %bitcast.9), calls=%async_computation | async-start | bytes 1048576 | tf_op jit(solution)/shard_map/all_to_all | solution.py:487
  47.6 13.9 %copy-start = (f32[1024]{0:T(1024)S(1)}, f32[1024]{0:T(1024)}, u32[]{:S(2)}) copy-start(f32[1024]{0:T(1024)} %param.18) | copy-start | bytes 12292
  52.7 36.0 %all-to-all-start.1 = ((bf16[1536,2,128]{2,1,0:T(2,128)(2,1)}), bf16[1536,2,128]{2,1,0:T(2,128)(2,1)S(1)}, u32[]{:S(2)}, u32[]{:S(2)}) async-start(bf16[1536,2,128]{2,1,0:T(2,128)(2,1)} %bitcast.11), calls=%async_computation.1 | async-start | bytes 1572864 | tf_op jit(solution)/shard_map/all_to_all | solution.py:487

commit v5 on v4

--- a/solution.py
+++ b/solution.py
@@ -11,7 +11,6 @@
 from jax.sharding import PartitionSpec as P
 
 LANES = 128
-GROUP = 8
 PACK_PARTS = 4
 VMEM_LIMIT = 16 * 1024 * 1024
 F32 = jnp.float32
@@ -106,8 +105,6 @@
             copy.start()
     owner_copy.wait()
     spots = owner_order(owner_in[...], holders)
-    place = iota((channels, LANES), 0).astype(F32)
-    lines = [jnp.where(place == spot, 1.0, 0.0).astype(B16) for spot in spots]
     for line, spot in enumerate(spots):
         spot_ref[line : line + 1, :] = spot
     spot_ref[len(spots) :, :] = owner_in[...].astype(F32)
@@ -118,14 +115,17 @@
         rows = slice(part * step, (part + 1) * step)
         back = (cot_in[rows, :].astype(F32) * gate_in[rows, :].astype(F32)).astype(B16)
         values.append(jnp.concatenate([sig_in[rows, :], back], axis=1))
-    moved = jnp.dot(
-        jnp.concatenate(lines, axis=1), jnp.concatenate(values, axis=0), preferred_element_type=F32
-    )
-    for side in range(2):
-        rows = slice(side * half, (side + 1) * half)
-        wide[pl.ds(side, half, stride=4), :] = moved[rows, 0:LANES]
-        wide[pl.ds(2 + side, half, stride=4), :] = moved[rows, LANES:]
+    values = jnp.concatenate(values, axis=0)
+    few = step // 2
     for part in range(PACK_PARTS):
+        place = iota((few, LANES), 0) + part * few
+        place = jnp.concatenate([place, place + half], axis=0).astype(F32)
+        lines = [jnp.where(place == spot, 1.0, 0.0).astype(B16) for spot in spots]
+        moved = jnp.dot(jnp.concatenate(lines, axis=1), values, preferred_element_type=F32)
+        for side in range(2):
+            rows = slice(side * few, (side + 1) * few)
+            wide[pl.ds(4 * few * part + side, few, stride=4), :] = moved[rows, 0:LANES]
+            wide[pl.ds(4 * few * part + 2 + side, few, stride=4), :] = moved[rows, LANES:]
         rows = slice(part * 2 * step, (part + 1) * 2 * step)
         out[rows, :] = wide[rows, :].astype(B16)
         write(part).start()
@@ -252,162 +252,143 @@
     )(place, emb, w_in, w_mid, w_out, rate, length, spots)
 
 
-def diagonal(upper, lower, key):
+def diagonal(here, after, key):
     total = None
     for a in range(LANES // 8):
         rows = slice(8 * a, 8 * a + 8)
-        piece = upper[rows, :] if lower is None else lower[rows, :]
-        if lower is None:
-            piece = jnp.where(key >= LANES - 1 - 8 * a, piece, 0.0)
-        else:
-            piece = jnp.where(key >= LANES - 1 - 8 * a, upper[rows, :], piece)
+        late = 0.0 if after is None else after[rows, :]
+        piece = jnp.where(key >= LANES - 8 * a, late, here[rows, :])
         if a:
             piece = pltpu.roll(piece, 8 * a, 1)
         total = piece if total is None else total + piece
-    total = pltpu.roll(total, 1, 1, stride=1, stride_axis=0)
+    total = pltpu.roll(total, 0, 1, stride=1, stride_axis=0)
     return jnp.sum(total, axis=0, keepdims=True)
 
 
-def convolve_body(
-    own_ref, arr_ref, ahead_ref, out_hbm, done_ref, wide, sig, back, y_acc, z_acc, lags, out, out_sem, *, norm
-):
+def convolve_body(own_ref, arr_ref, ahead_ref, out, wide, sig, back, lags, spread, *, norm):
     peers = arr_ref.shape[0] // 4
     blocks = ahead_ref.shape[0] // (2 * LANES)
     batch = peers // blocks
-    pad = (GROUP - 1) * batch
+    pairs = blocks // 2
+    count = pairs * batch
+    pad = sig.shape[2] - count
+    part = pairs // 2
     flip = flip_matrix()
+    same = (iota((LANES, LANES), 0) == iota((LANES, LANES), 1)).astype(F32).astype(B16)
     key = iota((8, LANES), 0) + iota((8, LANES), 1)
-    wide[0 : 4 * peers, :] = arr_ref[...].astype(F32)
+    wide[...] = arr_ref[...].astype(F32)
     zero = jnp.zeros((pad, LANES), B16)
+    empty = jnp.zeros((LANES, LANES), B16)
+
     for c in range(2):
-        sig[c, 0:pad, :] = zero
-        sig[c, pad : pad + peers, :] = wide[pl.ds(c, peers, stride=4), :].astype(B16)
-        back[c, 0:peers, :] = wide[pl.ds(2 + c, peers, stride=4), :].astype(B16)
-        back[c, peers : peers + pad, :] = zero
+        x = wide[pl.ds(c, peers, stride=4), :].astype(B16).reshape(pairs, 2, batch, LANES)
+        b = jnp.dot(wide[pl.ds(2 + c, peers, stride=4), :].astype(B16), flip, preferred_element_type=F32)
+        b = b.astype(B16).reshape(pairs, 2, batch, LANES)
+        for e in range(2):
+            sig[c, e, 0:pad, :] = zero
+            sig[c, e, pad:, :] = x[:, e].reshape(count, LANES)
+            back[c, e, 0:count, :] = b[:, e].reshape(count, LANES)
+            back[c, e, count:, :] = zero
+
+    def send(c, row, first, value):
+        for i in range(value.shape[0] // batch):
+            for e in range(2):
+                peer = (2 * (first + i) + e) * batch
+                spread[pl.ds(6 * peer + row + c, batch, stride=6), :] = value[
+                    i * batch : (i + 1) * batch, e * LANES : (e + 1) * LANES
+                ]
+
     for c in range(2):
-        turned = lax.dot_general(
-            flip, sig[c, pad : pad + peers, :], (((1,), (1,)), ((), ())), preferred_element_type=F32
-        ).astype(B16)
+
+        def table(k):
+            spot = (c * blocks + k) * LANES
+            return ahead_ref[spot : spot + LANES, :] if k >= 0 else empty
+
+        def grid(*tables):
+            rows = [jnp.concatenate([table(k) for k in line], axis=1) for line in tables]
+            return jnp.concatenate(rows, axis=0)
+
+        def earlier(first, m):
+            rows = slice(pad + (first - m) * batch, pad + (first - m + part) * batch)
+            return [sig[c, 0, rows, :], sig[c, 1, rows, :]]
+
+        def later(first, m):
+            rows = slice((first + m) * batch, (first + m + part) * batch)
+            return [back[c, 0, rows, :], back[c, 1, rows, :]]
+
+        turned = [
+            lax.dot_general(same, sig[c, e, pad:, :], (((1,), (1,)), ((), ())), preferred_element_type=F32).astype(B16)
+            for e in range(2)
+        ]
+        for first in range(0, pairs, part):
+            deep = range(first + part)
+            left = jnp.concatenate([piece for m in deep for piece in earlier(first, m)], axis=1)
+            right = [grid((2 * m, 2 * m + 1), (2 * m - 1, 2 * m)) for m in deep]
+            send(c, 0, first, jnp.dot(left, jnp.concatenate(right, axis=0), preferred_element_type=F32))
+            deep = range(pairs - first)
+            left = jnp.concatenate([piece for m in deep for piece in later(first, m)], axis=1)
+            right = [grid((2 * m, 2 * m - 1), (2 * m + 1, 2 * m)) for m in deep]
+            send(c, 2, first, jnp.dot(left, jnp.concatenate(right, axis=0), preferred_element_type=F32))
         before = None
-        for first in range(0, blocks, GROUP):
-            rows = (blocks - first) * batch
-            spots = slice((c * blocks + first) * LANES, (c * blocks + first + GROUP) * LANES)
-            left = jnp.concatenate(
-                [sig[c, pad - j * batch : pad - j * batch + rows, :] for j in range(GROUP)], axis=1
-            )
-            moved = jnp.concatenate(
-                [back[c, (first + j) * batch : (first + j) * batch + rows, :] for j in range(GROUP)], axis=1
-            )
-            y = jnp.dot(left, ahead_ref[spots, :], preferred_element_type=F32)
-            table = jnp.concatenate(
-                [ahead_ref[spots.start + j * LANES : spots.start + (j + 1) * LANES, :] for j in range(GROUP)], axis=1
-            )
-            z = lax.dot_general(moved, table, (((1,), (1,)), ((), ())), preferred_element_type=F32)
-            if first == 0:
-                y_acc[c] = y
-                z_acc[c] = z
-            else:
-                y_acc[c, first * batch :, :] += y
-                z_acc[c, 0:rows, :] += z
-            outer = jnp.dot(turned[:, 0:rows], moved, preferred_element_type=F32)
-            for j in range(GROUP):
+        for first in range(0, pairs, 4):
+            rows = count if first < part else count // 2
+            upper = []
+            lower = []
+            for m in range(first, first + 4):
+                here = slice(m * batch, m * batch + rows)
+                next_ = slice((m + 1) * batch, (m + 1) * batch + rows)
+                upper += [back[c, 0, here, :], back[c, 1, here, :]]
+                lower += [back[c, 1, here, :], back[c, 0, next_, :]]
+            right = jnp.concatenate([jnp.concatenate(upper, axis=1), jnp.concatenate(lower, axis=1)], axis=0)
+            left = jnp.concatenate([side[:, 0:rows] for side in turned], axis=1)
+            outer = jnp.dot(left, right, preferred_element_type=F32)
+            for j in range(8):
                 now = outer[:, j * LANES : (j + 1) * LANES]
                 if before is not None:
-                    lags[c * blocks + first + j - 1 : c * blocks + first + j, :] = diagonal(before, now, key)
+                    spot = c * blocks + 2 * first + j - 1
+                    lags[spot : spot + 1, :] = diagonal(before, now, key)
                 before = now
-        lags[c * blocks + blocks - 1 : c * blocks + blocks, :] = diagonal(before, None, key)
+        lags[(c + 1) * blocks - 1 : (c + 1) * blocks, :] = diagonal(before, None, key)
     point = (iota((blocks, LANES), 0) * LANES + iota((blocks, LANES), 1)).astype(F32)
     holder = jnp.concatenate([jnp.full((batch, LANES), h, jnp.int32) for h in range(blocks)], axis=0).astype(F32)
+    ordered = jnp.dot((lags[...] * norm).astype(B16), flip, preferred_element_type=F32)
     for c in range(2):
-        wide[pl.ds(c, peers, stride=6), :] = y_acc[c]
-        wide[pl.ds(2 + c, peers, stride=6), :] = z_acc[c]
         here = slice(c * blocks, (c + 1) * blocks)
-        lags[here, :] = jnp.where(point < own_ref[c : c + 1, :], lags[here, :] * norm, 0.0)
+        lags[here, :] = jnp.where(point < own_ref[c : c + 1, :], ordered[here, :], 0.0)
     for half in range(2):
         total = jnp.zeros((peers, LANES), F32)
         for c in range(2):
             column = lags[pl.ds(c * blocks + half, batch, stride=2), :]
             column = jnp.concatenate([column] * blocks, axis=0)
             total = jnp.where(holder == own_ref[2 + c : 3 + c, :], column, total)
-        wide[pl.ds(4 + half, peers, stride=6), :] = total
-    step = 6 * peers // PACK_PARTS
-
-    def write(part):
-        rows = pl.ds(part * step, step)
-        return pltpu.make_async_copy(out.at[rows, :], out_hbm.at[rows, :], out_sem.at[part])
-
-    for part in range(PACK_PARTS):
-        rows = slice(part * step, (part + 1) * step)
-        out[rows, :] = wide[rows, :].astype(B16)
-        write(part).start()
-    done_ref[...] = own_ref[...]
-    for part in range(PACK_PARTS):
-        write(part).wait()
+        spread[pl.ds(4 + half, peers, stride=6), :] = total
+    out[...] = spread[...].astype(B16)
 
 
 def convolve(own, arrived, ahead, norm):
     peers = arrived.shape[0] // 4
     blocks = ahead.shape[0] // (2 * LANES)
-    pad = (GROUP - 1) * (peers // blocks)
+    rows = peers // 2 + LANES
     body = lambda *refs: convolve_body(*refs, norm=norm)
     return pl.pallas_call(
         body,
         in_specs=[VM, VM, VM],
-        out_specs=(HB, VM),
-        out_shape=(jax.ShapeDtypeStruct((6 * peers, LANES), B16), jax.ShapeDtypeStruct(own.shape, F32)),
+        out_specs=VM,
+        out_shape=jax.ShapeDtypeStruct((6 * peers, LANES), B16),
         scratch_shapes=[
+            pltpu.VMEM((4 * peers, LANES), F32),
+            pltpu.VMEM((2, 2, rows, LANES), B16),
+            pltpu.VMEM((2, 2, rows, LANES), B16),
+            pltpu.VMEM((2 * blocks, LANES), F32),
             pltpu.VMEM((6 * peers, LANES), F32),
-            pltpu.VMEM((2, peers + pad, LANES), B16),
-            pltpu.VMEM((2, peers + pad, LANES), B16),
-            pltpu.VMEM((2, peers, LANES), F32),
-            pltpu.VMEM((2, peers, LANES), F32),
-            pltpu.VMEM((2 * blocks, LANES), F32),
-            pltpu.VMEM((6 * peers, LANES), B16),
-            pltpu.SemaphoreType.DMA((PACK_PARTS,)),
         ],
         compiler_params=PARAMS,
         name="convolve",
     )(own, arrived, ahead)
 
 
-def route_body(
-    after_ref, spot_ref, skip_ref, sig_hbm, gate_hbm, cot_hbm, out_ref, direct_ref, pulled_ref, gate_ref, cot_ref, sig_ref, in_sem
-):
-    pairs = ((sig_hbm, sig_ref), (gate_hbm, gate_ref), (cot_hbm, cot_ref))
-    copies = [pltpu.make_async_copy(src, dst, in_sem.at[which]) for which, (src, dst) in enumerate(pairs)]
-    for copy in copies:
-        copy.start()
-
-    def turned(ref, line):
-        return jnp.broadcast_to(ref[line : line + 1, :], (LANES, LANES)).T
-
-    for line in range(skip_ref.shape[0]):
-        out_ref[line * LANES : (line + 1) * LANES, :] = turned(spot_ref, line)
-    for copy in copies:
-        copy.wait()
-    for line in range(skip_ref.shape[0]):
-        rows = slice(line * LANES, (line + 1) * LANES)
-        skip = turned(skip_ref, line)
-        direct_ref[rows, :] = skip * sig_ref[rows, :].astype(F32)
-        pulled_ref[rows, :] = skip * (cot_ref[rows, :].astype(F32) * gate_ref[rows, :].astype(F32))
-
-
-def route(after, spots, skip, sig, gate, cot):
-    data = jax.ShapeDtypeStruct(sig.shape, B16)
-    wide = jax.ShapeDtypeStruct(sig.shape, F32)
-    return pl.pallas_call(
-        route_body,
-        in_specs=[VM] * 3 + [HB] * 3,
-        out_specs=(VM,) * 5,
-        out_shape=(wide, wide, wide, data, data),
-        scratch_shapes=[pltpu.VMEM(sig.shape, B16), pltpu.SemaphoreType.DMA((3,))],
-        compiler_params=PARAMS,
-        name="route",
-    )(after, spots, skip.reshape(-1, LANES), *far(sig, gate, cot))
-
-
 def finish_body(
-    me_ref, ret_ref, route_ref, direct_ref, pulled_ref, gate_ref, cot_ref, spot_ref,
+    me_ref, ret_ref, sig_ref, gate_ref, cot_ref, skip_ref, spot_ref,
     result_hbm, d_gate_hbm, d_sig_hbm, grad_ref, wide, result, d_gate, d_sig, out_sem
 ):
     wide[...] = ret_ref[...].astype(F32)
@@ -417,7 +398,12 @@
     def take(row):
         return wide[pl.ds(row, half, stride=6), :].astype(B16)
 
-    sides = [jnp.concatenate([take(c), take(2 + c)], axis=1) for c in range(2)]
+    flip = flip_matrix()
+
+    def ordered(row):
+        return jnp.dot(take(row), flip, preferred_element_type=F32).astype(B16)
+
+    sides = [jnp.concatenate([take(c), ordered(2 + c)], axis=1) for c in range(2)]
     arrived = jnp.concatenate(sides, axis=0)
     step = channels // PACK_PARTS
     pairs = ((result, result_hbm), (d_gate, d_gate_hbm), (d_sig, d_sig_hbm))
@@ -430,15 +416,24 @@
         ]
 
     lane = iota((step, LANES), 1).astype(F32)
+
+    def turned(ref, part):
+        few = step // LANES
+        lines = [jnp.broadcast_to(ref[part * few + i : part * few + i + 1, :], (LANES, LANES)).T for i in range(few)]
+        return jnp.concatenate(lines, axis=0)
+
     for part in range(PACK_PARTS):
         rows = slice(part * step, (part + 1) * step)
-        spot = route_ref[rows, :]
+        spot = turned(spot_ref, part)
+        skip = turned(skip_ref, part)
+        gate = gate_ref[rows, :].astype(F32)
+        cot = cot_ref[rows, :].astype(F32)
         lines = [jnp.where(lane + line * LANES == spot, 1.0, 0.0).astype(B16) for line in range(channels // LANES)]
         both = jnp.dot(jnp.concatenate(lines, axis=1), arrived, preferred_element_type=F32)
-        mixed = both[:, 0:LANES] + direct_ref[rows, :]
-        result[rows, :] = (gate_ref[rows, :].astype(F32) * mixed).astype(B16)
-        d_gate[rows, :] = (cot_ref[rows, :].astype(F32) * mixed).astype(B16)
-        d_sig[rows, :] = (pulled_ref[rows, :] + both[:, LANES:]).astype(B16)
+        mixed = both[:, 0:LANES] + skip * sig_ref[rows, :].astype(F32)
+        result[rows, :] = (gate * mixed).astype(B16)
+        d_gate[rows, :] = (cot * mixed).astype(B16)
+        d_sig[rows, :] = (skip * (cot * gate) + both[:, LANES:]).astype(B16)
         for copy in writes(part):
             copy.start()
 
@@ -462,13 +457,12 @@
             copy.wait()
 
 
-def finish(me, returned, routed, spots, slots):
-    gate = routed[3]
+def finish(me, returned, sig, gate, cot, skip, spots, slots):
     data = jax.ShapeDtypeStruct(gate.shape, B16)
     held = pltpu.VMEM(gate.shape, B16)
     return pl.pallas_call(
         finish_body,
-        in_specs=[SM] + [VM] * 7,
+        in_specs=[SM] + [VM] * 6,
         out_specs=(HB, HB, HB, VM),
         out_shape=(data, data, data, jax.ShapeDtypeStruct((slots, 2 * LANES), F32)),
         scratch_shapes=[
@@ -480,7 +474,7 @@
         ],
         compiler_params=PARAMS,
         name="finish",
-    )(me, returned, *routed, spots)
+    )(me, returned, sig, gate, cot, skip.reshape(-1, LANES), spots)
 
 
 def exchange(array, rows):
@@ -512,11 +506,10 @@
     ahead, own = make_tables(
         place.reshape(1).astype(jnp.int32), jnp.asarray(table), w_in_wide, w_mid, w_out, rates, lengths, spots
     )
-    outs, done = convolve(own, arrived, ahead, norm)
-    routed = route(done, spots, skip, sig, gat, cot)
+    outs = convolve(own, arrived, ahead, norm)
     returned = exchange(outs, 2)
     result, d_gate, d_signal, tap_grad = finish(
-        ctx_place.reshape(1).astype(jnp.int32), returned, routed, spots, 2 * channels // ctx_count
+        ctx_place.reshape(1).astype(jnp.int32), returned, sig, gat, cot, skip, spots, 2 * channels // ctx_count
     )
     return (result[None], d_gate[None], d_signal[None], tap_grad)
 

time: 91.5 us -> 90.4 us (0.988)
  blocking collectives: 0 us -> 36.3 us
  waiting for transfers between devices: 40.6 us -> 14.8 us
  starting transfers between devices: 31 us -> 22.2 us
  Pallas kernels: 17.9 us -> 15.1 us
    all_to_all x0 -> x1, blocking collectives: none -> 36.3 us  [exchange(): lax.all_to_all(array.reshape(-1, rows, LANES), ('ctx', 'dp'), split_axis=...]
    all_to_all x2 -> x1, waiting for transfers between devices: 40.6 us -> 14.8 us  [exchange(): lax.all_to_all(array.reshape(-1, rows, LANES), ('ctx', 'dp'), split_axis=...]
    all_to_all x2 -> x1, starting transfers between devices: 31 us -> 22.2 us  [exchange(): lax.all_to_all(array.reshape(-1, rows, LANES), ('ctx', 'dp'), split_axis=...]
    pallas_call x3 -> x2, Pallas kernels: 8.79 us -> 5.95 us  [the longest x1 3.44 us: convolve(): pl.pallas_call(body, in_specs=[VM, VM, VM], out_specs=VM, out_shape=jax.S...]
  transfers between devices with their start and end apart: 2 -> 1, of which waited for: 2 -> 1; matrix products, arithmetic and copies ran while one was open for 1% -> 1% of each run, Pallas kernels for 8% -> 7%
where the time goes in v5:
time: 90.4 us; the launch traced here: 90.1 us
  blocking collectives  36.3 us (40%)
  starting transfers between devices  22.2 us (25%)
  Pallas kernels  15.1 us (17%)
  waiting for transfers between devices  14.8 us (16%)
    all_to_all x1, blocking collectives, exchange(): lax.all_to_all(array.reshape(-1, rows, LANES), ('ctx', 'dp'), split_axis=...  36.3 us
    all_to_all x1, starting transfers between devices, exchange(): lax.all_to_all(array.reshape(-1, rows, LANES), ('ctx', 'dp'), split_axis=...  22.2 us
    all_to_all x1, waiting for transfers between devices, exchange(): lax.all_to_all(array.reshape(-1, rows, LANES), ('ctx', 'dp'), split_axis=...  14.8 us
    pallas_call x1, Pallas kernels, make_tables(): pl.pallas_call(tables_body, in_specs=[SM, HB, VM, HB, HB, HB, HB, VM], ou...  6.21 us
    pallas_call x1, Pallas kernels, convolve(): pl.pallas_call(body, in_specs=[VM, VM, VM], out_specs=VM, out_shape=jax.S...  3.44 us
    pallas_call x1, Pallas kernels, pack(): pl.pallas_call(lambda *refs: pack_body(*refs, holders=holders), in_specs=...  2.98 us
    pallas_call x1, Pallas kernels, finish(): pl.pallas_call(finish_body, in_specs=[SM] + [VM] * 6, out_specs=(HB, HB,...  2.51 us
  transfers between devices with their start and end apart: 1, of which 1 were waited for; matrix products, arithmetic and copies ran while one was open for 1% of the time, Pallas kernels for 7%

profile of v5, /device:TPU:1, one launch (start us, length us, event | category | flops | bytes accessed | tf_op | source)
XLA Modules:
  0.0 90.1 jit_solution(3740376511964557979)
XLA Ops:
  0.6 3.0 %pack.1 = (bf16[2048,128]{1,0:T(8,128)(2,1)}, f32[16,128]{1,0:T(8,128)S(1)}) custom-call(s32[8,128]{1,0:T(8,128)} %bitcast.28, bf16[1024,128]{1,0:T(8,128)(2,1)} %bitcast.20, bf16[1024,128]{1,0:T(8,128)(2,1)} %bitcast.22, bf16[1024,128]{1,0:T(8,128)(2,1)} %bitcast.24), custom_call_target="tpu_custom_call" | custom-call | tf_op jit(solution)/shard_map/pack/pallas_call | solution.py:140
  3.6 22.2 %all-to-all-start = ((bf16[512,4,128]{2,1,0:T(4,128)(2,1)}), bf16[512,4,128]{2,1,0:T(4,128)(2,1)S(1)}, u32[]{:S(2)}, u32[]{:S(2)}) async-start(bf16[512,4,128]{2,1,0:T(4,128)(2,1)} %bitcast.9), calls=%async_computation | async-start | bytes 1048576 | tf_op jit(solution)/shard_map/all_to_all | solution.py:481
  25.8 0.8 copy.15
  26.6 6.2 %tables.1 = (bf16[8192,128]{1,0:T(8,128)(2,1)S(1)}, f32[8,128]{1,0:T(8,128)S(1)}) custom-call(s32[1]{0:T(128)} %bitcast.1.place_ref, bf16[48,4096]{1,0:T(8,128)(2,1)} %constant.16.clone.emb_hbm, bf16[64,48]{1,0:T(8,128)(2,1)S(1)} %pad.4.w_in_ref, bf16[64,64]{1,0:T(8,128)(2,1)} %w_mid_hbm.1, bf16[64,1024]{1,0:T(8,128)(2,1)} %bitcast.27, f32[8,128]{1,0:T(8,128)} %bitcast.29, ...), custom_call_target="tpu_custom_call" | custom-call | tf_op jit(solution)/shard_map/tables/pallas_call | solution.py:241
  32.8 14.8 %all-to-all-done = bf16[512,4,128]{2,1,0:T(4,128)(2,1)S(1)} async-done(((bf16[512,4,128]{2,1,0:T(4,128)(2,1)}), bf16[512,4,128]{2,1,0:T(4,128)(2,1)S(1)}, u32[]{:S(2)}, u32[]{:S(2)}) %all-to-all-start) | async-done | bytes 524320 | tf_op jit(solution)/shard_map/all_to_all | solution.py:481
  47.7 0.0 copy-start
  47.7 0.0 copy-start.1
  47.7 0.0 copy-start.2
  47.7 0.0 copy-start.3
  47.7 3.4 %convolve.1 = bf16[3072,128]{1,0:T(8,128)(2,1)S(1)} custom-call(f32[8,128]{1,0:T(8,128)S(1)} %get-tuple-element.13.refs_0_, bf16[2048,128]{1,0:T(8,128)(2,1)S(1)} %bitcast.19, bf16[8192,128]{1,0:T(8,128)(2,1)S(1)} %get-tuple-element.15.refs_2_), custom_call_target="tpu_custom_call" | custom-call | tf_op jit(solution)/shard_map/convolve/pallas_call | solution.py:373
  51.1 36.3 %all_to_all.10 = bf16[1536,2,128]{2,1,0:T(2,128)(2,1)S(1)} all-to-all(bf16[1536,2,128]{2,1,0:T(2,128)(2,1)S(1)} %bitcast.18), channel_id=1, replica_groups=mesh['dp'=16,'ctx'=32] {'ctx','dp'}, dimensions={0} | all-to-all | bytes 1572864 | tf_op jit(solution)/shard_map/all_to_all | solution.py:481
  87.4 0.0 copy-done
  87.4 0.0 copy-done.1
  87.4 0.0 copy-done.2
  87.4 0.0 copy-done.3
  87.4 2.5 %finish.1 = (bf16[1024,128]{1,0:T(8,128)(2,1)}, bf16[1024,128]{1,0:T(8,128)(2,1)}, bf16[1024,128]{1,0:T(8,128)(2,1)}, f32[64,256]{1,0:T(8,128)}) custom-call(s32[1]{0:T(128)} %bitcast.me_ref, bf16[3072,128]{1,0:T(8,128)(2,1)S(1)} %bitcast.17, bf16[1024,128]{1,0:T(8,128)(2,1)S(1)} %bitcast.21, bf16[1024,128]{1,0:T(8,128)(2,1)S(1)} %bitcast.23, ...), custom_call_target="tpu_custom_call" | custom-call | tf_op jit(solution)/shard_map/finish/pallas_call | solution.py:463
  (1 shorter events, 0.0 us)
Async XLA Ops:
  3.6 44.0 %all-to-all-start = ((bf16[512,4,128]{2,1,0:T(4,128)(2,1)}), bf16[512,4,128]{2,1,0:T(4,128)(2,1)S(1)}, u32[]{:S(2)}, u32[]{:S(2)}) async-start(bf16[512,4,128]{2,1,0:T(4,128)(2,1)} %bitcast.9), calls=%async_computation | async-start | bytes 1048576 | tf_op jit(solution)/shard_map/all_to_all | solution.py:481
  47.7 39.7 %copy-start = (bf16[1,1024,128]{2,1,0:T(8,128)(2,1)S(1)}, bf16[1,1024,128]{2,1,0:T(8,128)(2,1)}, u32[]{:S(2)}) copy-start(bf16[1,1024,128]{2,1,0:T(8,128)(2,1)} %param.11) | copy-start | bytes 786436
  47.7 39.7 %copy-start.1 = (bf16[1,1024,128]{2,1,0:T(8,128)(2,1)S(1)}, bf16[1,1024,128]{2,1,0:T(8,128)(2,1)}, u32[]{:S(2)}) copy-start(bf16[1,1024,128]{2,1,0:T(8,128)(2,1)} %param.12) | copy-start | bytes 786436
  47.7 39.7 %copy-start.2 = (bf16[1,1024,128]{2,1,0:T(8,128)(2,1)S(1)}, bf16[1,1024,128]{2,1,0:T(8,128)(2,1)}, u32[]{:S(2)}) copy-start(bf16[1,1024,128]{2,1,0:T(8,128)(2,1)} %param.13) | copy-start | bytes 786436
  47.7 39.7 %copy-start.3 = (f32[1024]{0:T(1024)S(1)}, f32[1024]{0:T(1024)}, u32[]{:S(2)}) copy-start(f32[1024]{0:T(1024)} %param.18) | copy-start | bytes 12292

commit v6 on v5

--- a/solution.py
+++ b/solution.py
@@ -87,12 +87,7 @@
     step = channels // PACK_PARTS
     pairs = ((sig_hbm, sig_in), (gate_hbm, gate_in), (cot_hbm, cot_in))
 
-    def reads(part):
-        rows = pl.ds(part * step, step)
-        return [
-            pltpu.make_async_copy(src.at[rows, :], dst.at[rows, :], in_sem.at[part * 3 + which])
-            for which, (src, dst) in enumerate(pairs)
-        ]
+    reads = [pltpu.make_async_copy(src, dst, in_sem.at[which]) for which, (src, dst) in enumerate(pairs)]
 
     def write(part):
         rows = pl.ds(part * 2 * step, 2 * step)
@@ -100,28 +95,34 @@
 
     owner_copy = pltpu.make_async_copy(owner_hbm, owner_in, owner_sem.at[0])
     owner_copy.start()
-    for part in range(PACK_PARTS):
-        for copy in reads(part):
-            copy.start()
+    for copy in reads:
+        copy.start()
     owner_copy.wait()
     spots = owner_order(owner_in[...], holders)
     for line, spot in enumerate(spots):
         spot_ref[line : line + 1, :] = spot
     spot_ref[len(spots) :, :] = owner_in[...].astype(F32)
-    values = []
+    for copy in reads:
+        copy.wait()
+    back = (cot_in[...].astype(F32) * gate_in[...].astype(F32)).astype(B16)
+    values = jnp.concatenate([sig_in[...], back], axis=1)
+    few = step // 2
+    row = iota((LANES, LANES), 0).astype(F32).astype(B16)
+    one = jnp.ones((LANES, LANES), B16)
+    none = jnp.zeros((LANES, LANES), B16)
+
+    def onehot(block, spot):
+        low = spot - block * LANES
+        low = jnp.where((low >= 0) & (low < LANES), low, 2.0 * LANES).astype(B16)
+        return jnp.where(row == low, one, none)
+
     for part in range(PACK_PARTS):
-        for copy in reads(part):
-            copy.wait()
-        rows = slice(part * step, (part + 1) * step)
-        back = (cot_in[rows, :].astype(F32) * gate_in[rows, :].astype(F32)).astype(B16)
-        values.append(jnp.concatenate([sig_in[rows, :], back], axis=1))
-    values = jnp.concatenate(values, axis=0)
-    few = step // 2
-    for part in range(PACK_PARTS):
-        place = iota((few, LANES), 0) + part * few
-        place = jnp.concatenate([place, place + half], axis=0).astype(F32)
-        lines = [jnp.where(place == spot, 1.0, 0.0).astype(B16) for spot in spots]
-        moved = jnp.dot(jnp.concatenate(lines, axis=1), values, preferred_element_type=F32)
+        chosen = []
+        for side in range(2):
+            for block in range(few // LANES):
+                block += (side * half + part * few) // LANES
+                chosen.append(jnp.concatenate([onehot(block, spot) for spot in spots], axis=1))
+        moved = jnp.dot(jnp.concatenate(chosen, axis=0), values, preferred_element_type=F32)
         for side in range(2):
             rows = slice(side * few, (side + 1) * few)
             wide[pl.ds(4 * few * part + side, few, stride=4), :] = moved[rows, 0:LANES]
@@ -150,7 +151,7 @@
             pltpu.VMEM((rows, LANES), F32),
             pltpu.VMEM((rows, LANES), B16),
             pltpu.SemaphoreType.DMA((1,)),
-            pltpu.SemaphoreType.DMA((3 * PACK_PARTS,)),
+            pltpu.SemaphoreType.DMA((3,)),
             pltpu.SemaphoreType.DMA((PACK_PARTS,)),
         ],
         compiler_params=PARAMS,
@@ -188,7 +189,7 @@
     length = chosen(len_ref)
     own_ref[0:2, :] = jnp.broadcast_to(length[0:2, :], (2, LANES))
     own_ref[2:4, :] = jnp.broadcast_to(chosen(spot_ref, lines)[0:2, :], (2, LANES))
-    own_ref[4:8, :] = jnp.zeros((4, LANES), F32)
+    own_ref[4:8, :] = jnp.full((4, LANES), place_ref[1], jnp.int32).astype(F32)
     scale = lax.rsqrt(jnp.maximum(length, 1.0))
     w_in = w_in_ref[...]
     w_mid = w_mid_ref[...]
@@ -388,8 +389,8 @@
 
 
 def finish_body(
-    me_ref, ret_ref, sig_ref, gate_ref, cot_ref, skip_ref, spot_ref,
-    result_hbm, d_gate_hbm, d_sig_hbm, grad_ref, wide, result, d_gate, d_sig, out_sem
+    own_ref, ret_ref, sig_ref, gate_ref, cot_ref, skip_ref, spot_ref,
+    result_hbm, d_gate_hbm, d_sig_hbm, grad_hbm, wide, result, d_gate, d_sig, grad, out_sem, grad_sem
 ):
     wide[...] = ret_ref[...].astype(F32)
     channels = gate_ref.shape[0]
@@ -415,7 +416,25 @@
             for which, (src, dst) in enumerate(pairs)
         ]
 
+    def tally(hits):
+        lanes = jnp.sum(hits.astype(F32), axis=0, keepdims=True)
+        return jnp.sum(lanes, axis=1, keepdims=True)
+
+    slots = grad.shape[0]
+    owner = spot_ref[spot_ref.shape[0] // 2 :, :]
+    me = own_ref[4:5, :]
+    slot = iota((slots, half), 0).astype(F32)
+    first = tally(owner < me)
+    count = tally(owner == me)
+    source = slot + first
+    source = jnp.where(source >= half, source - half, source)
+    chosen = jnp.where((iota((slots, half), 1).astype(F32) == source) & (slot < count), 1.0, 0.0).astype(B16)
+    table = jnp.concatenate([take(4), take(5)], axis=1)
+    grad[...] = jnp.dot(chosen, table, preferred_element_type=F32)
+    grad_copy = pltpu.make_async_copy(grad, grad_hbm, grad_sem.at[0])
+    grad_copy.start()
     lane = iota((step, LANES), 1).astype(F32)
+    none = jnp.zeros((step, LANES), B16)
 
     def turned(ref, part):
         few = step // LANES
@@ -428,7 +447,10 @@
         skip = turned(skip_ref, part)
         gate = gate_ref[rows, :].astype(F32)
         cot = cot_ref[rows, :].astype(F32)
-        lines = [jnp.where(lane + line * LANES == spot, 1.0, 0.0).astype(B16) for line in range(channels // LANES)]
+        block = jnp.floor(spot * (1.0 / LANES))
+        mark = jnp.where(lane == spot - block * LANES, 1.0, 0.0).astype(B16)
+        block = block.astype(B16)
+        lines = [jnp.where(block == line, mark, none) for line in range(channels // LANES)]
         both = jnp.dot(jnp.concatenate(lines, axis=1), arrived, preferred_element_type=F32)
         mixed = both[:, 0:LANES] + skip * sig_ref[rows, :].astype(F32)
         result[rows, :] = (gate * mixed).astype(B16)
@@ -437,44 +459,32 @@
         for copy in writes(part):
             copy.start()
 
-    def tally(hits):
-        lanes = jnp.sum(hits.astype(F32), axis=0, keepdims=True)
-        return jnp.sum(lanes, axis=1, keepdims=True)
-
-    slots = grad_ref.shape[0]
-    owner = spot_ref[spot_ref.shape[0] // 2 :, :]
-    me = me_ref[0].astype(F32)
-    slot = iota((slots, half), 0).astype(F32)
-    first = tally(owner < me)
-    count = tally(owner == me)
-    source = slot + first
-    source = jnp.where(source >= half, source - half, source)
-    chosen = jnp.where((iota((slots, half), 1).astype(F32) == source) & (slot < count), 1.0, 0.0).astype(B16)
-    table = jnp.concatenate([take(4), take(5)], axis=1)
-    grad_ref[...] = jnp.dot(chosen, table, preferred_element_type=F32)
     for part in range(PACK_PARTS):
         for copy in writes(part):
             copy.wait()
-
-
-def finish(me, returned, sig, gate, cot, skip, spots, slots):
+    grad_copy.wait()
+
+
+def finish(own, returned, sig, gate, cot, skip, spots, slots):
     data = jax.ShapeDtypeStruct(gate.shape, B16)
     held = pltpu.VMEM(gate.shape, B16)
     return pl.pallas_call(
         finish_body,
-        in_specs=[SM] + [VM] * 6,
-        out_specs=(HB, HB, HB, VM),
+        in_specs=[VM] * 7,
+        out_specs=(HB,) * 4,
         out_shape=(data, data, data, jax.ShapeDtypeStruct((slots, 2 * LANES), F32)),
         scratch_shapes=[
             pltpu.VMEM(returned.shape, F32),
             held,
             held,
             held,
+            pltpu.VMEM((slots, 2 * LANES), F32),
             pltpu.SemaphoreType.DMA((3 * PACK_PARTS,)),
+            pltpu.SemaphoreType.DMA((1,)),
         ],
         compiler_params=PARAMS,
         name="finish",
-    )(me, returned, sig, gate, cot, skip.reshape(-1, LANES), spots)
+    )(own, returned, sig, gate, cot, skip.reshape(-1, LANES), spots)
 
 
 def exchange(array, rows):
@@ -504,12 +514,12 @@
     table[:features] = embed_table(seq_len, features)
     w_in_wide = jnp.pad(w_in, ((0, 0), (0, padded - features)))
     ahead, own = make_tables(
-        place.reshape(1).astype(jnp.int32), jnp.asarray(table), w_in_wide, w_mid, w_out, rates, lengths, spots
+        jnp.stack([place, ctx_place]).astype(jnp.int32), jnp.asarray(table), w_in_wide, w_mid, w_out, rates, lengths, spots
     )
     outs = convolve(own, arrived, ahead, norm)
     returned = exchange(outs, 2)
     result, d_gate, d_signal, tap_grad = finish(
-        ctx_place.reshape(1).astype(jnp.int32), returned, sig, gat, cot, skip, spots, 2 * channels // ctx_count
+        own, returned, sig, gat, cot, skip, spots, 2 * channels // ctx_count
     )
     return (result[None], d_gate[None], d_signal[None], tap_grad)
 

time: 90.4 us -> 89.4 us (0.989)
  transfers between devices with their start and end apart: 1 -> 1, of which waited for: 1 -> 1; matrix products, arithmetic and copies ran while one was open for 1% -> 1% of each run, Pallas kernels for 7% -> 8%
where the time goes in v6:
time: 89.4 us; the launch traced here: 89.1 us
  blocking collectives  36.3 us (41%)
  starting transfers between devices  22.2 us (25%)
  Pallas kernels  14.7 us (16%)
  waiting for transfers between devices  14.2 us (16%)
    all_to_all x1, blocking collectives, exchange(): lax.all_to_all(array.reshape(-1, rows, LANES), ('ctx', 'dp'), split_axis=...  36.3 us
    all_to_all x1, starting transfers between devices, exchange(): lax.all_to_all(array.reshape(-1, rows, LANES), ('ctx', 'dp'), split_axis=...  22.2 us
    all_to_all x1, waiting for transfers between devices, exchange(): lax.all_to_all(array.reshape(-1, rows, LANES), ('ctx', 'dp'), split_axis=...  14.2 us
    pallas_call x1, Pallas kernels, make_tables(): pl.pallas_call(tables_body, in_specs=[SM, HB, VM, HB, HB, HB, HB, VM], ou...  6.75 us
    pallas_call x1, Pallas kernels, convolve(): pl.pallas_call(body, in_specs=[VM, VM, VM], out_specs=VM, out_shape=jax.S...  3.44 us
    pallas_call x1, Pallas kernels, pack(): pl.pallas_call(lambda *refs: pack_body(*refs, holders=holders), in_specs=...  2.68 us
    pallas_call x1, Pallas kernels, finish(): pl.pallas_call(finish_body, in_specs=[VM] * 7, out_specs=(HB,) * 4, out_s...  1.83 us
  transfers between devices with their start and end apart: 1, of which 1 were waited for; matrix products, arithmetic and copies ran while one was open for 1% of the time, Pallas kernels for 8%

profile of v6, /device:TPU:1, one launch (start us, length us, event | category | flops | bytes accessed | tf_op | source)
XLA Modules:
  0.0 89.1 jit_solution(16611731310191352272)
XLA Ops:
  0.6 2.7 %pack.1 = (bf16[2048,128]{1,0:T(8,128)(2,1)}, f32[16,128]{1,0:T(8,128)S(1)}) custom-call(s32[8,128]{1,0:T(8,128)} %bitcast.28, bf16[1024,128]{1,0:T(8,128)(2,1)} %bitcast.20, bf16[1024,128]{1,0:T(8,128)(2,1)} %bitcast.22, bf16[1024,128]{1,0:T(8,128)(2,1)} %bitcast.24), custom_call_target="tpu_custom_call" | custom-call | tf_op jit(solution)/shard_map/pack/pallas_call | solution.py:141
  3.3 22.2 %all-to-all-start = ((bf16[512,4,128]{2,1,0:T(4,128)(2,1)}), bf16[512,4,128]{2,1,0:T(4,128)(2,1)S(1)}, u32[]{:S(2)}, u32[]{:S(2)}) async-start(bf16[512,4,128]{2,1,0:T(4,128)(2,1)} %bitcast.9), calls=%async_computation | async-start | bytes 1048576 | tf_op jit(solution)/shard_map/all_to_all | solution.py:491
  25.5 0.8 copy.15
  26.3 0.1 pad_add_fusion.place_ref
  26.4 6.7 %tables.1 = (bf16[8192,128]{1,0:T(8,128)(2,1)S(1)}, f32[8,128]{1,0:T(8,128)S(1)}) custom-call(s32[2]{0:T(128)S(1)} %pad_add_fusion.place_ref, bf16[48,4096]{1,0:T(8,128)(2,1)} %constant.16.clone.emb_hbm, bf16[64,48]{1,0:T(8,128)(2,1)S(1)} %pad.4.w_in_ref, bf16[64,64]{1,0:T(8,128)(2,1)} %w_mid_hbm.1, bf16[64,1024]{1,0:T(8,128)(2,1)} %bitcast.27, ...), custom_call_target="tpu_custom_call" | custom-call | tf_op jit(solution)/shard_map/tables/pallas_call | solution.py:242
  33.2 14.2 %all-to-all-done = bf16[512,4,128]{2,1,0:T(4,128)(2,1)S(1)} async-done(((bf16[512,4,128]{2,1,0:T(4,128)(2,1)}), bf16[512,4,128]{2,1,0:T(4,128)(2,1)S(1)}, u32[]{:S(2)}, u32[]{:S(2)}) %all-to-all-start) | async-done | bytes 524320 | tf_op jit(solution)/shard_map/all_to_all | solution.py:491
  47.4 0.0 copy-start
  47.4 0.0 copy-start.1
  47.4 0.0 copy-start.2
  47.4 0.0 copy-start.3
  47.4 3.4 %convolve.1 = bf16[3072,128]{1,0:T(8,128)(2,1)S(1)} custom-call(f32[8,128]{1,0:T(8,128)S(1)} %get-tuple-element.13.refs_0_.own_ref, bf16[2048,128]{1,0:T(8,128)(2,1)S(1)} %bitcast.19, bf16[8192,128]{1,0:T(8,128)(2,1)S(1)} %get-tuple-element.15.refs_2_), custom_call_target="tpu_custom_call" | custom-call | tf_op jit(solution)/shard_map/convolve/pallas_call | solution.py:374
  50.8 36.3 %all_to_all.10 = bf16[1536,2,128]{2,1,0:T(2,128)(2,1)S(1)} all-to-all(bf16[1536,2,128]{2,1,0:T(2,128)(2,1)S(1)} %bitcast.18), channel_id=1, replica_groups=mesh['dp'=16,'ctx'=32] {'ctx','dp'}, dimensions={0} | all-to-all | bytes 1572864 | tf_op jit(solution)/shard_map/all_to_all | solution.py:491
  87.1 0.0 copy-done
  87.1 0.0 copy-done.1
  87.1 0.0 copy-done.2
  87.1 0.0 copy-done.3
  87.1 1.8 %finish.1 = (bf16[1024,128]{1,0:T(8,128)(2,1)}, bf16[1024,128]{1,0:T(8,128)(2,1)}, bf16[1024,128]{1,0:T(8,128)(2,1)}, f32[64,256]{1,0:T(8,128)}) custom-call(f32[8,128]{1,0:T(8,128)S(1)} %get-tuple-element.13.refs_0_.own_ref, bf16[3072,128]{1,0:T(8,128)(2,1)S(1)} %bitcast.17, bf16[1024,128]{1,0:T(8,128)(2,1)S(1)} %bitcast.21, ...), custom_call_target="tpu_custom_call" | custom-call | tf_op jit(solution)/shard_map/finish/pallas_call | solution.py:471
  (1 shorter events, 0.0 us)
Async XLA Ops:
  3.3 44.0 %all-to-all-start = ((bf16[512,4,128]{2,1,0:T(4,128)(2,1)}), bf16[512,4,128]{2,1,0:T(4,128)(2,1)S(1)}, u32[]{:S(2)}, u32[]{:S(2)}) async-start(bf16[512,4,128]{2,1,0:T(4,128)(2,1)} %bitcast.9), calls=%async_computation | async-start | bytes 1048576 | tf_op jit(solution)/shard_map/all_to_all | solution.py:491
  47.4 39.7 %copy-start = (bf16[1,1024,128]{2,1,0:T(8,128)(2,1)S(1)}, bf16[1,1024,128]{2,1,0:T(8,128)(2,1)}, u32[]{:S(2)}) copy-start(bf16[1,1024,128]{2,1,0:T(8,128)(2,1)} %param.11) | copy-start | bytes 786436
  47.4 39.7 %copy-start.1 = (bf16[1,1024,128]{2,1,0:T(8,128)(2,1)S(1)}, bf16[1,1024,128]{2,1,0:T(8,128)(2,1)}, u32[]{:S(2)}) copy-start(bf16[1,1024,128]{2,1,0:T(8,128)(2,1)} %param.12) | copy-start | bytes 786436
  47.4 39.7 %copy-start.2 = (bf16[1,1024,128]{2,1,0:T(8,128)(2,1)S(1)}, bf16[1,1024,128]{2,1,0:T(8,128)(2,1)}, u32[]{:S(2)}) copy-start(bf16[1,1024,128]{2,1,0:T(8,128)(2,1)} %param.13) | copy-start | bytes 786436
  47.4 39.7 %copy-start.3 = (f32[1024]{0:T(1024)S(1)}, f32[1024]{0:T(1024)}, u32[]{:S(2)}) copy-start(f32[1024]{0:T(1024)} %param.18) | copy-start | bytes 12292

commit v7 on v6

--- a/solution.py
+++ b/solution.py
@@ -321,15 +321,6 @@
             lax.dot_general(same, sig[c, e, pad:, :], (((1,), (1,)), ((), ())), preferred_element_type=F32).astype(B16)
             for e in range(2)
         ]
-        for first in range(0, pairs, part):
-            deep = range(first + part)
-            left = jnp.concatenate([piece for m in deep for piece in earlier(first, m)], axis=1)
-            right = [grid((2 * m, 2 * m + 1), (2 * m - 1, 2 * m)) for m in deep]
-            send(c, 0, first, jnp.dot(left, jnp.concatenate(right, axis=0), preferred_element_type=F32))
-            deep = range(pairs - first)
-            left = jnp.concatenate([piece for m in deep for piece in later(first, m)], axis=1)
-            right = [grid((2 * m, 2 * m - 1), (2 * m + 1, 2 * m)) for m in deep]
-            send(c, 2, first, jnp.dot(left, jnp.concatenate(right, axis=0), preferred_element_type=F32))
         before = None
         for first in range(0, pairs, 4):
             rows = count if first < part else count // 2
@@ -350,6 +341,15 @@
                     lags[spot : spot + 1, :] = diagonal(before, now, key)
                 before = now
         lags[(c + 1) * blocks - 1 : (c + 1) * blocks, :] = diagonal(before, None, key)
+        for first in range(0, pairs, part):
+            deep = range(first + part)
+            left = jnp.concatenate([piece for m in deep for piece in earlier(first, m)], axis=1)
+            right = [grid((2 * m, 2 * m + 1), (2 * m - 1, 2 * m)) for m in deep]
+            send(c, 0, first, jnp.dot(left, jnp.concatenate(right, axis=0), preferred_element_type=F32))
+            deep = range(pairs - first)
+            left = jnp.concatenate([piece for m in deep for piece in later(first, m)], axis=1)
+            right = [grid((2 * m, 2 * m - 1), (2 * m + 1, 2 * m)) for m in deep]
+            send(c, 2, first, jnp.dot(left, jnp.concatenate(right, axis=0), preferred_element_type=F32))
     point = (iota((blocks, LANES), 0) * LANES + iota((blocks, LANES), 1)).astype(F32)
     holder = jnp.concatenate([jnp.full((batch, LANES), h, jnp.int32) for h in range(blocks)], axis=0).astype(F32)
     ordered = jnp.dot((lags[...] * norm).astype(B16), flip, preferred_element_type=F32)

time: 89.4 us -> 89.2 us (level)
  no operation moved by 1% of the time
where the time goes in v7:
time: 89.2 us; the launch traced here: 88.9 us
  blocking collectives  36.3 us (41%)
  starting transfers between devices  22.2 us (25%)
  Pallas kernels  14.5 us (16%)
  waiting for transfers between devices  14.2 us (16%)
    all_to_all x1, blocking collectives, exchange(): lax.all_to_all(array.reshape(-1, rows, LANES), ('ctx', 'dp'), split_axis=...  36.3 us
    all_to_all x1, starting transfers between devices, exchange(): lax.all_to_all(array.reshape(-1, rows, LANES), ('ctx', 'dp'), split_axis=...  22.2 us
    all_to_all x1, waiting for transfers between devices, exchange(): lax.all_to_all(array.reshape(-1, rows, LANES), ('ctx', 'dp'), split_axis=...  14.2 us
    pallas_call x1, Pallas kernels, make_tables(): pl.pallas_call(tables_body, in_specs=[SM, HB, VM, HB, HB, HB, HB, VM], ou...  6.75 us
    pallas_call x1, Pallas kernels, convolve(): pl.pallas_call(body, in_specs=[VM, VM, VM], out_specs=VM, out_shape=jax.S...  3.21 us
    pallas_call x1, Pallas kernels, pack(): pl.pallas_call(lambda *refs: pack_body(*refs, holders=holders), in_specs=...  2.68 us
    pallas_call x1, Pallas kernels, finish(): pl.pallas_call(finish_body, in_specs=[VM] * 7, out_specs=(HB,) * 4, out_s...  1.83 us
  transfers between devices with their start and end apart: 1, of which 1 were waited for; matrix products, arithmetic and copies ran while one was open for 1% of the time, Pallas kernels for 8%

profile of v7, /device:TPU:1, one launch (start us, length us, event | category | flops | bytes accessed | tf_op | source)
XLA Modules:
  0.0 88.9 jit_solution(15130277453307728325)
XLA Ops:
  0.6 2.7 %pack.1 = (bf16[2048,128]{1,0:T(8,128)(2,1)}, f32[16,128]{1,0:T(8,128)S(1)}) custom-call(s32[8,128]{1,0:T(8,128)} %bitcast.28, bf16[1024,128]{1,0:T(8,128)(2,1)} %bitcast.20, bf16[1024,128]{1,0:T(8,128)(2,1)} %bitcast.22, bf16[1024,128]{1,0:T(8,128)(2,1)} %bitcast.24), custom_call_target="tpu_custom_call" | custom-call | tf_op jit(solution)/shard_map/pack/pallas_call | solution.py:141
  3.3 22.2 %all-to-all-start = ((bf16[512,4,128]{2,1,0:T(4,128)(2,1)}), bf16[512,4,128]{2,1,0:T(4,128)(2,1)S(1)}, u32[]{:S(2)}, u32[]{:S(2)}) async-start(bf16[512,4,128]{2,1,0:T(4,128)(2,1)} %bitcast.9), calls=%async_computation | async-start | bytes 1048576 | tf_op jit(solution)/shard_map/all_to_all | solution.py:491
  25.5 0.8 copy.15
  26.3 0.1 pad_add_fusion.place_ref
  26.4 6.7 %tables.1 = (bf16[8192,128]{1,0:T(8,128)(2,1)S(1)}, f32[8,128]{1,0:T(8,128)S(1)}) custom-call(s32[2]{0:T(128)S(1)} %pad_add_fusion.place_ref, bf16[48,4096]{1,0:T(8,128)(2,1)} %constant.16.clone.emb_hbm, bf16[64,48]{1,0:T(8,128)(2,1)S(1)} %pad.4.w_in_ref, bf16[64,64]{1,0:T(8,128)(2,1)} %w_mid_hbm.1, bf16[64,1024]{1,0:T(8,128)(2,1)} %bitcast.27, ...), custom_call_target="tpu_custom_call" | custom-call | tf_op jit(solution)/shard_map/tables/pallas_call | solution.py:242
  33.2 14.2 %all-to-all-done = bf16[512,4,128]{2,1,0:T(4,128)(2,1)S(1)} async-done(((bf16[512,4,128]{2,1,0:T(4,128)(2,1)}), bf16[512,4,128]{2,1,0:T(4,128)(2,1)S(1)}, u32[]{:S(2)}, u32[]{:S(2)}) %all-to-all-start) | async-done | bytes 524320 | tf_op jit(solution)/shard_map/all_to_all | solution.py:491
  47.4 0.0 copy-start
  47.4 0.0 copy-start.1
  47.4 0.0 copy-start.2
  47.4 0.0 copy-start.3
  47.4 3.2 %convolve.1 = bf16[3072,128]{1,0:T(8,128)(2,1)S(1)} custom-call(f32[8,128]{1,0:T(8,128)S(1)} %get-tuple-element.13.refs_0_.own_ref, bf16[2048,128]{1,0:T(8,128)(2,1)S(1)} %bitcast.19, bf16[8192,128]{1,0:T(8,128)(2,1)S(1)} %get-tuple-element.15.refs_2_), custom_call_target="tpu_custom_call" | custom-call | tf_op jit(solution)/shard_map/convolve/pallas_call | solution.py:374
  50.6 36.3 %all_to_all.10 = bf16[1536,2,128]{2,1,0:T(2,128)(2,1)S(1)} all-to-all(bf16[1536,2,128]{2,1,0:T(2,128)(2,1)S(1)} %bitcast.18), channel_id=1, replica_groups=mesh['dp'=16,'ctx'=32] {'ctx','dp'}, dimensions={0} | all-to-all | bytes 1572864 | tf_op jit(solution)/shard_map/all_to_all | solution.py:491
  86.9 0.0 copy-done
  86.9 0.0 copy-done.1
  86.9 0.0 copy-done.2
  86.9 0.0 copy-done.3
  86.9 1.8 %finish.1 = (bf16[1024,128]{1,0:T(8,128)(2,1)}, bf16[1024,128]{1,0:T(8,128)(2,1)}, bf16[1024,128]{1,0:T(8,128)(2,1)}, f32[64,256]{1,0:T(8,128)}) custom-call(f32[8,128]{1,0:T(8,128)S(1)} %get-tuple-element.13.refs_0_.own_ref, bf16[3072,128]{1,0:T(8,128)(2,1)S(1)} %bitcast.17, bf16[1024,128]{1,0:T(8,128)(2,1)S(1)} %bitcast.21, ...), custom_call_target="tpu_custom_call" | custom-call | tf_op jit(solution)/shard_map/finish/pallas_call | solution.py:471
  (1 shorter events, 0.0 us)
Async XLA Ops:
  3.3 44.0 %all-to-all-start = ((bf16[512,4,128]{2,1,0:T(4,128)(2,1)}), bf16[512,4,128]{2,1,0:T(4,128)(2,1)S(1)}, u32[]{:S(2)}, u32[]{:S(2)}) async-start(bf16[512,4,128]{2,1,0:T(4,128)(2,1)} %bitcast.9), calls=%async_computation | async-start | bytes 1048576 | tf_op jit(solution)/shard_map/all_to_all | solution.py:491
  47.4 39.5 %copy-start = (bf16[1,1024,128]{2,1,0:T(8,128)(2,1)S(1)}, bf16[1,1024,128]{2,1,0:T(8,128)(2,1)}, u32[]{:S(2)}) copy-start(bf16[1,1024,128]{2,1,0:T(8,128)(2,1)} %param.11) | copy-start | bytes 786436
  47.4 39.5 %copy-start.1 = (bf16[1,1024,128]{2,1,0:T(8,128)(2,1)S(1)}, bf16[1,1024,128]{2,1,0:T(8,128)(2,1)}, u32[]{:S(2)}) copy-start(bf16[1,1024,128]{2,1,0:T(8,128)(2,1)} %param.12) | copy-start | bytes 786436
  47.4 39.5 %copy-start.2 = (bf16[1,1024,128]{2,1,0:T(8,128)(2,1)S(1)}, bf16[1,1024,128]{2,1,0:T(8,128)(2,1)}, u32[]{:S(2)}) copy-start(bf16[1,1024,128]{2,1,0:T(8,128)(2,1)} %param.13) | copy-start | bytes 786436
  47.4 39.5 %copy-start.3 = (f32[1024]{0:T(1024)S(1)}, f32[1024]{0:T(1024)}, u32[]{:S(2)}) copy-start(f32[1024]{0:T(1024)} %param.18) | copy-start | bytes 12292

commit v8 on v7

--- a/solution.py
+++ b/solution.py
@@ -275,7 +275,6 @@
     pad = sig.shape[2] - count
     part = pairs // 2
     flip = flip_matrix()
-    same = (iota((LANES, LANES), 0) == iota((LANES, LANES), 1)).astype(F32).astype(B16)
     key = iota((8, LANES), 0) + iota((8, LANES), 1)
     wide[...] = arr_ref[...].astype(F32)
     zero = jnp.zeros((pad, LANES), B16)
@@ -317,10 +316,7 @@
             rows = slice((first + m) * batch, (first + m + part) * batch)
             return [back[c, 0, rows, :], back[c, 1, rows, :]]
 
-        turned = [
-            lax.dot_general(same, sig[c, e, pad:, :], (((1,), (1,)), ((), ())), preferred_element_type=F32).astype(B16)
-            for e in range(2)
-        ]
+        turned = [sig[c, e, pad:, :].astype(F32).T.astype(B16) for e in range(2)]
         before = None
         for first in range(0, pairs, 4):
             rows = count if first < part else count // 2

time: 89.2 us -> 89 us (level)
  no operation moved by 1% of the time
where the time goes in v8:
time: 89 us; the launch traced here: 88.7 us
  blocking collectives  36.3 us (41%)
  starting transfers between devices  22.2 us (25%)
  Pallas kernels  14.3 us (16%)
  waiting for transfers between devices  14.2 us (16%)
    all_to_all x1, blocking collectives, exchange(): lax.all_to_all(array.reshape(-1, rows, LANES), ('ctx', 'dp'), split_axis=...  36.3 us
    all_to_all x1, starting transfers between devices, exchange(): lax.all_to_all(array.reshape(-1, rows, LANES), ('ctx', 'dp'), split_axis=...  22.2 us
    all_to_all x1, waiting for transfers between devices, exchange(): lax.all_to_all(array.reshape(-1, rows, LANES), ('ctx', 'dp'), split_axis=...  14.2 us
    pallas_call x1, Pallas kernels, make_tables(): pl.pallas_call(tables_body, in_specs=[SM, HB, VM, HB, HB, HB, HB, VM], ou...  6.75 us
    pallas_call x1, Pallas kernels, convolve(): pl.pallas_call(body, in_specs=[VM, VM, VM], out_specs=VM, out_shape=jax.S...  3.04 us
    pallas_call x1, Pallas kernels, pack(): pl.pallas_call(lambda *refs: pack_body(*refs, holders=holders), in_specs=...  2.68 us
    pallas_call x1, Pallas kernels, finish(): pl.pallas_call(finish_body, in_specs=[VM] * 7, out_specs=(HB,) * 4, out_s...  1.83 us
  transfers between devices with their start and end apart: 1, of which 1 were waited for; matrix products, arithmetic and copies ran while one was open for 1% of the time, Pallas kernels for 8%

profile of v8, /device:TPU:1, one launch (start us, length us, event | category | flops | bytes accessed | tf_op | source)
XLA Modules:
  0.0 88.7 jit_solution(5205745287238925136)
XLA Ops:
  0.6 2.7 %pack.1 = (bf16[2048,128]{1,0:T(8,128)(2,1)}, f32[16,128]{1,0:T(8,128)S(1)}) custom-call(s32[8,128]{1,0:T(8,128)} %bitcast.28, bf16[1024,128]{1,0:T(8,128)(2,1)} %bitcast.20, bf16[1024,128]{1,0:T(8,128)(2,1)} %bitcast.22, bf16[1024,128]{1,0:T(8,128)(2,1)} %bitcast.24), custom_call_target="tpu_custom_call" | custom-call | tf_op jit(solution)/shard_map/pack/pallas_call | solution.py:141
  3.3 22.2 %all-to-all-start = ((bf16[512,4,128]{2,1,0:T(4,128)(2,1)}), bf16[512,4,128]{2,1,0:T(4,128)(2,1)S(1)}, u32[]{:S(2)}, u32[]{:S(2)}) async-start(bf16[512,4,128]{2,1,0:T(4,128)(2,1)} %bitcast.9), calls=%async_computation | async-start | bytes 1048576 | tf_op jit(solution)/shard_map/all_to_all | solution.py:487
  25.5 0.8 copy.15
  26.3 0.1 pad_add_fusion.place_ref
  26.4 6.7 %tables.1 = (bf16[8192,128]{1,0:T(8,128)(2,1)S(1)}, f32[8,128]{1,0:T(8,128)S(1)}) custom-call(s32[2]{0:T(128)S(1)} %pad_add_fusion.place_ref, bf16[48,4096]{1,0:T(8,128)(2,1)} %constant.16.clone.emb_hbm, bf16[64,48]{1,0:T(8,128)(2,1)S(1)} %pad.4.w_in_ref, bf16[64,64]{1,0:T(8,128)(2,1)} %w_mid_hbm.1, bf16[64,1024]{1,0:T(8,128)(2,1)} %bitcast.27, ...), custom_call_target="tpu_custom_call" | custom-call | tf_op jit(solution)/shard_map/tables/pallas_call | solution.py:242
  33.2 14.2 %all-to-all-done = bf16[512,4,128]{2,1,0:T(4,128)(2,1)S(1)} async-done(((bf16[512,4,128]{2,1,0:T(4,128)(2,1)}), bf16[512,4,128]{2,1,0:T(4,128)(2,1)S(1)}, u32[]{:S(2)}, u32[]{:S(2)}) %all-to-all-start) | async-done | bytes 524320 | tf_op jit(solution)/shard_map/all_to_all | solution.py:487
  47.4 0.0 copy-start
  47.4 0.0 copy-start.1
  47.4 0.0 copy-start.2
  47.4 0.0 copy-start.3
  47.4 3.0 %convolve.1 = bf16[3072,128]{1,0:T(8,128)(2,1)S(1)} custom-call(f32[8,128]{1,0:T(8,128)S(1)} %get-tuple-element.13.refs_0_.own_ref, bf16[2048,128]{1,0:T(8,128)(2,1)S(1)} %bitcast.19, bf16[8192,128]{1,0:T(8,128)(2,1)S(1)} %get-tuple-element.15.refs_2_), custom_call_target="tpu_custom_call" | custom-call | tf_op jit(solution)/shard_map/convolve/pallas_call | solution.py:370
  50.4 36.3 %all_to_all.10 = bf16[1536,2,128]{2,1,0:T(2,128)(2,1)S(1)} all-to-all(bf16[1536,2,128]{2,1,0:T(2,128)(2,1)S(1)} %bitcast.18), channel_id=1, replica_groups=mesh['dp'=16,'ctx'=32] {'ctx','dp'}, dimensions={0} | all-to-all | bytes 1572864 | tf_op jit(solution)/shard_map/all_to_all | solution.py:487
  86.7 0.0 copy-done
  86.7 0.0 copy-done.1
  86.7 0.0 copy-done.2
  86.7 0.0 copy-done.3
  86.7 1.8 %finish.1 = (bf16[1024,128]{1,0:T(8,128)(2,1)}, bf16[1024,128]{1,0:T(8,128)(2,1)}, bf16[1024,128]{1,0:T(8,128)(2,1)}, f32[64,256]{1,0:T(8,128)}) custom-call(f32[8,128]{1,0:T(8,128)S(1)} %get-tuple-element.13.refs_0_.own_ref, bf16[3072,128]{1,0:T(8,128)(2,1)S(1)} %bitcast.17, bf16[1024,128]{1,0:T(8,128)(2,1)S(1)} %bitcast.21, ...), custom_call_target="tpu_custom_call" | custom-call | tf_op jit(solution)/shard_map/finish/pallas_call | solution.py:467
  (1 shorter events, 0.0 us)
Async XLA Ops:
  3.3 44.0 %all-to-all-start = ((bf16[512,4,128]{2,1,0:T(4,128)(2,1)}), bf16[512,4,128]{2,1,0:T(4,128)(2,1)S(1)}, u32[]{:S(2)}, u32[]{:S(2)}) async-start(bf16[512,4,128]{2,1,0:T(4,128)(2,1)} %bitcast.9), calls=%async_computation | async-start | bytes 1048576 | tf_op jit(solution)/shard_map/all_to_all | solution.py:487
  47.4 39.3 %copy-start = (bf16[1,1024,128]{2,1,0:T(8,128)(2,1)S(1)}, bf16[1,1024,128]{2,1,0:T(8,128)(2,1)}, u32[]{:S(2)}) copy-start(bf16[1,1024,128]{2,1,0:T(8,128)(2,1)} %param.11) | copy-start | bytes 786436
  47.4 39.3 %copy-start.1 = (bf16[1,1024,128]{2,1,0:T(8,128)(2,1)S(1)}, bf16[1,1024,128]{2,1,0:T(8,128)(2,1)}, u32[]{:S(2)}) copy-start(bf16[1,1024,128]{2,1,0:T(8,128)(2,1)} %param.12) | copy-start | bytes 786436
  47.4 39.3 %copy-start.2 = (bf16[1,1024,128]{2,1,0:T(8,128)(2,1)S(1)}, bf16[1,1024,128]{2,1,0:T(8,128)(2,1)}, u32[]{:S(2)}) copy-start(bf16[1,1024,128]{2,1,0:T(8,128)(2,1)} %param.13) | copy-start | bytes 786436
  47.4 39.3 %copy-start.3 = (f32[1024]{0:T(1024)S(1)}, f32[1024]{0:T(1024)}, u32[]{:S(2)}) copy-start(f32[1024]{0:T(1024)} %param.18) | copy-start | bytes 12292
